TPU v7x, 128 devices: a whole 4x4x4 slice. The times are simulated.
128 devices in a mesh: walk: 4 (over x_lo, core), chol: 32 (over y, z, x_hi).
Axes of the slice: x: 4 (x_hi: 2, x_lo: 2; x = x_hi * 2 + x_lo), y: 4, z: 4, core: 2. Of those that a mesh axis runs over, the one named last changes fastest.
Arguments:
- walkers: bfloat16 [8, 32, 1024, 256], P('walk', 'chol'), may hold values from -1 to 2
- counts: int32 [8, 32], P('walk', 'chol'), may hold values from 0 to 3, as said below
- slot_copy: int32 [8, 32], P('walk', 'chol'), may hold values from 0 to 7, as said below
- factors: bfloat16 [32, 256, 1024], P('chol'), may hold values from -1 to 1
Outputs:
- combed: bfloat16 [8, 32, 1024, 256], P('walk', 'chol')
- gradient: float32 [8, 32, 1024, 256], P('walk', 'chol')
Inputs may be any that keep to these rules, and one draw needn't show every extreme that they name: In each population (column) the counts sum to 8. `slot_copy`: each column is a permutation of the copy numbers 0 to 7.
All inputs are finite; a program needn't handle non-finite values.
Results may differ from a plain program's by a relative error of at most 0.0068.
Values may be sent and summed in bfloat16 or wider, within the bound.
No kernel may reach another device: no remote copies, remote signals or barrier semaphores. Data moves between devices by JAX's collectives and lax.ppermute only.
A program may use at most 64 MiB of HBM per device.

v0:
```python
import jax
import jax.numpy as jnp
from jax import lax
from jax.sharding import PartitionSpec as P

NEL = 256
NEWTON = 8


def shard_term(factor_block, green_block):
    rotated = jnp.einsum(
        "lrm,wmq->wlrq", factor_block, green_block, preferred_element_type=jnp.float32
    ).astype(jnp.bfloat16)
    shard_grad = -jnp.einsum(
        "lam,wlia->wmi", factor_block, rotated, preferred_element_type=jnp.float32
    )
    return lax.optimization_barrier(shard_grad.astype(jnp.bfloat16)).astype(jnp.float32)


def body(walkers, counts, slot_copy, factors):
    pop_counts = lax.all_gather(counts, "walk", axis=0, tiled=True)
    inclusive = jnp.cumsum(pop_counts[:, 0])
    wanted = slot_copy[:, 0]
    source = jnp.sum((inclusive[None, :] <= wanted[:, None]).astype(jnp.int32), axis=1)
    arrived = lax.all_gather(walkers, "walk", axis=0, tiled=True)
    height = arrived.shape[0]
    inside = (source >= 0) & (source < height)
    chosen = jnp.take(arrived, jnp.clip(source, 0, height - 1), axis=0)
    combed = jnp.where(inside[:, None, None, None], chosen, jnp.zeros_like(walkers))
    squares = combed[:, 0]
    intersection = squares[:, :NEL, :].astype(jnp.float32)
    identity = jnp.eye(NEL, dtype=jnp.float32)
    inverse = jnp.broadcast_to(identity, intersection.shape)
    for newton_step in range(NEWTON):
        product = jnp.einsum("wij,wjk->wik", intersection, inverse, precision=lax.Precision.HIGHEST)
        inverse = jnp.einsum(
            "wij,wjk->wik", inverse, 2.0 * identity - product, precision=lax.Precision.HIGHEST
        )
    green_block = jnp.einsum(
        "wmj,wji->wmi", squares, inverse.astype(jnp.bfloat16), preferred_element_type=jnp.float32
    ).astype(jnp.bfloat16)
    zero_grad = jnp.zeros(green_block.shape, jnp.float32)
    running = zero_grad
    shards = lax.all_gather(factors, "chol", axis=0, tiled=True).reshape((-1,) + factors.shape)

    def one_shard(partial_value, factor_block):
        return (partial_value + shard_term(factor_block, green_block), None)

    running, unused = lax.scan(one_shard, running, shards)
    return (combed, running[:, None])


def solution(mesh):
    in_specs = (
        P("walk", "chol", None, None),
        P("walk", "chol"),
        P("walk", "chol"),
        P("chol", None, None),
    )
    out_specs = (P("walk", "chol", None, None), P("walk", "chol", None, None))
    return jax.shard_map(body, mesh=mesh, in_specs=in_specs, out_specs=out_specs, check_vma=False)
```

profile of v0, /device:TPU:0, one launch (start us, length us, event | category | flops | bytes accessed | tf_op | source)
XLA Modules:
  0.0 324.4 jit_solution(11762103074547020921)
XLA Ops:
  11.3 5.0 %all-reduce = s32[8]{0:T(128)S(1)} all-reduce(s32[8]{0:T(128)S(1)} %bitcast_dynamic-update-slice_fusion), channel_id=1, replica_groups=mesh['walk'=4,'chol'=32] {'walk'}, use_global_device_ids=true, to_apply=%add | all-reduce | flops 8 | bytes 64
  18.1 39.8 %all-gather.3.cloned.1.call-done = bf16[8,1,1024,256]{3,2,1,0:T(8,128)(2,1)} async-done(((bf16[2,1,1024,256]{3,2,1,0:T(8,128)(2,1)}), bf16[8,1,1024,256]{3,2,1,0:T(8,128)(2,1)}) %all-gather.3.cloned.1.call-update) | async-done | bytes 4194320 | tf_op jit(solution)/shard_map/all_gather | solution.py:25
  58.0 2.8 gather_fusion
  73.1 145.7 %all-gather.5.cloned.1.call-done = bf16[32,256,1024]{2,1,0:T(8,128)(2,1)} async-done(((bf16[1,256,1024]{2,1,0:T(8,128)(2,1)}), bf16[32,256,1024]{2,1,0:T(8,128)(2,1)}) %all-gather.5.cloned.1.call-update) | async-done | bytes 16777232 | tf_op jit(solution)/shard_map/all_gather | solution.py:44
  218.8 96.9 %while.11 = (s32[]{:T(128)}, f32[2,1024,256]{1,2,0:T(8,128)S(1)}, bf16[32,1,256,1024]{3,2,1,0:T(8,128)(2,1)}, bf16[2,1024,256]{2,1,0:T(8,128)(2,1)}, s32[]{:T(128)}, /*index=5*/s32[]{:T(128)}) while((s32[]{:T(128)}, f32[2,1024,256]{1,2,0:T(8,128)S(1)}, bf16[32,1,256,1024]{3,2,1,0:T(8,128)(2,1)}, bf16[2,1024,256]{2,1,0:T(8,128)(2,1)}, ...), condition=%wide.region_3.4_spmd.clone, body=%wide.region_2.3_spmd.clone.sunk | while | flops 539623424 | bytes 8389719 | solution.py:49
  221.8 2.3 fusion.63
  227.8 2.3 fusion.63
  233.9 2.3 fusion.63
  237.0 2.3 fusion.63
  240.0 2.4 fusion.63
  243.1 2.3 fusion.63
  249.1 2.3 fusion.63
  252.1 2.3 fusion.63
  255.2 2.3 fusion.63
  258.2 2.3 fusion.63
  261.2 2.3 fusion.63
  264.3 2.3 fusion.63
  267.3 2.3 fusion.63
  276.4 2.3 fusion.63
  288.4 2.3 fusion.63
  294.5 2.4 fusion.63
  303.6 2.3 fusion.63
  306.6 2.3 fusion.63
  312.7 2.3 fusion.63
  (82 shorter events, 71.2 us)
Async XLA Ops:
  7.2 50.8 %all-gather.3.cloned.1.call-start = ((), (), s32[]{:S(2)}) async-start(), calls=%async_computation | async-start | bytes 5242880 | tf_op jit(solution)/shard_map/all_gather | solution.py:25
  7.9 210.9 %all-gather.5.cloned.1.call-start = ((), (), s32[]{:S(2)}) async-start(), calls=%async_computation.1 | async-start | bytes 17301504 | tf_op jit(solution)/shard_map/all_gather | solution.py:44
  60.8 1.0 copy-start
Sparse Core Ops, SparseCore 0:
  9.6 48.2 all-gather.2
  61.0 157.7 all-gather.4
where the time goes:
time: 326 us; the launch traced here: 324 us
  waiting for transfers between devices  187 us (57%)
  matrix products  84.2 us (26%)
  other arithmetic  25.1 us (8%)
  between operations  14.8 us (5%)
  local copies, waits for them, and re-layouts  7.37 us (2%)
  blocking collectives  5.01 us (2%)
    all_gather x1, waiting for transfers between devices, body(): lax.all_gather(factors, 'chol', axis=0, tiled=True)  146 us
    dot_general x32, matrix products, shard_term(): jnp.einsum('lam,wlia->wmi', factor_block, rotated, preferred_element_type...  74 us
    all_gather x1, waiting for transfers between devices, body(): arrived = lax.all_gather(walkers, 'walk', axis=0, tiled=True)  39.8 us
    add x32, other arithmetic, one_shard(): return (partial_value + shard_term(factor_block, green_block), None)  21.9 us
  transfers between devices with their start and end apart: 2, of which 2 were waited for; matrix products, arithmetic and copies ran while one was open for 6% of the time, Pallas kernels for 0%

commit v1 on v0

v1 whole, which is shorter than its diff:
```python
import functools

import jax
import jax.numpy as jnp
from jax import lax
from jax.experimental import pallas as pl
from jax.experimental.pallas import tpu as pltpu
from jax.sharding import PartitionSpec as P

NEL = 256
M = 1024
NEWTON = 8
MIB = 1 << 20


BF16 = jnp.bfloat16
F32 = jnp.float32
VM = pl.BlockSpec(memory_space=pltpu.VMEM)
SM = pl.BlockSpec(memory_space=pltpu.SMEM)


def dot(a, b):
    return jnp.dot(a, b, preferred_element_type=F32)


def line(x_lo, core, y, z, x_hi):
    return (x_lo * 2 + core) * 32 + (y * 4 + z) * 2 + x_hi


def moved(x, where):
    pairs = []
    for x_lo in range(2):
        for core in range(2):
            for y in range(4):
                for z in range(4):
                    for x_hi in range(2):
                        here = (x_lo, core, y, z, x_hi)
                        pairs.append((line(*here), line(*where(*here))))
    return lax.ppermute(x, ("walk", "chol"), pairs)


def to_core(x):
    return moved(x, lambda xl, c, y, z, xh: (xl, 1 - c, y, z, xh))


def to_pair(x):
    return moved(x, lambda xl, c, y, z, xh: (1 - xl, c, y, z, xh))


def swap_factor(x):
    def where(xl, c, y, z, xh):
        return (xl, c, y, z, xh) if c == xh else (1 - xl, 1 - c, y, z, 1 - xh)

    return moved(x, where)


def along_a(x, s):
    def where(xl, c, y, z, xh):
        return (xl, c, (y + s) % 4, z, xh) if c == 0 else (xl, c, y, (z + s) % 4, xh)

    return moved(x, where)


def along_b(x, s):
    def where(xl, c, y, z, xh):
        return (xl, c, y, (z + s) % 4, xh) if c == 0 else (xl, c, (y + s) % 4, z, xh)

    return moved(x, where)


def pick(source, refs, store):
    for j, ref in enumerate(refs):

        @pl.when((source >> 1) == j)
        def _():
            store(ref, source & 1)


def find_sources(my, refs, src_ref):
    info = [[ref[i, NEL : NEL + 16, 0:128].astype(F32) for i in range(2)] for ref in refs]
    count = {(r, i): info[r][i][0:1] for r in range(4) for i in range(2)}
    position = {(r, i): (my ^ r) * 2 + i for r in range(4) for i in range(2)}
    upto = {}
    for here in count:
        total = count[here]
        for there in count:
            if there != here:
                total = total + jnp.where(position[there] < position[here], count[there], 0.0)
        upto[here] = total
    found = []
    for s in range(4):
        slot = info[s // 2][s % 2][1:2]
        chosen = jnp.zeros_like(slot)
        for r, i in count:
            inside = (upto[r, i] > slot) & (upto[r, i] - count[r, i] <= slot)
            chosen = chosen + jnp.where(inside, float(2 * r + i), 0.0)
        found.append(jnp.max(chosen).astype(jnp.int32))
        src_ref[s] = found[s]
    return found


def newton_kernel(my_ref, own_ref, core_ref, pair_ref, diag_ref, src_ref, inv_ref, a_ref, x_ref, r_ref, z_ref):
    refs = (own_ref, core_ref, pair_ref, diag_ref)
    found = find_sources(my_ref[0], refs, src_ref)
    row = lax.broadcasted_iota(jnp.int32, (NEL, NEL), 0)
    col = lax.broadcasted_iota(jnp.int32, (NEL, NEL), 1)
    one = jnp.where(row == col, 1.0, 0.0).astype(F32)
    for s in range(4):

        def store(ref, i, s=s):
            a_ref[s] = ref[i, 0:NEL]

        pick(found[s], refs, store)

    def split(value, high, low):
        upper = value.astype(BF16)
        z_ref[high] = upper
        z_ref[low] = (value - upper.astype(F32)).astype(BF16)

    def blocks(s):
        at = s * 4
        return at, at + 1, at + 2, at + 3

    for s in range(4):
        xh, rh, xl, rl = blocks(s)
        residual = one - a_ref[s].astype(F32)
        split(residual, rh, rl)
        x_ref[s] = one + residual
    for s in range(4):
        xh, rh, xl, rl = blocks(s)
        r_ref[s] = dot(z_ref[rh], z_ref[rh]) + (dot(z_ref[rh], z_ref[rl]) + dot(z_ref[rl], z_ref[rh]))

    def step(k, carry):
        for s in range(4):
            xh, rh, xl, rl = blocks(s)
            split(x_ref[s], xh, xl)
            split(r_ref[s], rh, rl)
        for s in range(4):
            xh, rh, xl, rl = blocks(s)
            both = z_ref[xh : xh + 4].reshape(4 * NEL, NEL)
            by_high = dot(both, z_ref[rh])
            by_low = dot(both[: 2 * NEL], z_ref[rl])
            x_ref[s] = x_ref[s] + (by_high[:NEL] + (by_high[2 * NEL : 3 * NEL] + by_low[:NEL]))
            r_ref[s] = by_high[NEL : 2 * NEL] + (by_high[3 * NEL :] + by_low[NEL:])
        return carry

    lax.fori_loop(0, NEWTON - 2, step, 0)
    for s in range(4):
        xh, rh, xl, rl = blocks(s)
        split(x_ref[s], xh, xl)
        split(r_ref[s], rh, rl)
    for s in range(4):
        xh, rh, xl, rl = blocks(s)
        last = dot(z_ref[xh], z_ref[rh]) + (dot(z_ref[xh], z_ref[rl]) + dot(z_ref[xl], z_ref[rh]))
        inv_ref[s] = (x_ref[s] + last).astype(BF16)


def newton(my, own, core, pair, diag):
    return pl.pallas_call(
        newton_kernel,
        in_specs=[SM, VM, VM, VM, VM],
        out_specs=[SM, VM],
        out_shape=[
            jax.ShapeDtypeStruct((4,), jnp.int32),
            pltpu.VMEM((4, NEL, NEL), BF16),
        ],
        scratch_shapes=[
            pltpu.VMEM((4, NEL, NEL), BF16),
            pltpu.VMEM((4, NEL, NEL), F32),
            pltpu.VMEM((4, NEL, NEL), F32),
            pltpu.VMEM((16, NEL, NEL), BF16),
        ],
        compiler_params=pltpu.CompilerParams(vmem_limit_bytes=16 * MIB),
        name="newton",
    )(my, own, core, pair, diag)


def green_kernel(src_ref, own_ref, core_ref, pair_ref, diag_ref, inv_ref, *rest, at, rows):
    green_ref, new_ref, c_ref = rest[-3:]
    refs = (own_ref, core_ref, pair_ref, diag_ref)
    for s in range(4):

        def store(ref, i, s=s):
            if s < 2:
                new_ref[s, at : at + rows] = ref[i, 0:rows]
            else:
                c_ref[s - 2] = ref[i, 0:rows]

        pick(src_ref[s], refs, store)
    for s in range(4):
        c = new_ref[s, at : at + rows] if s < 2 else c_ref[s - 2]
        green_ref[s, at : at + rows] = dot(c, inv_ref[s]).astype(BF16)


def green_piece(src, own, core, pair, diag, inv, so_far, at, rows):
    carried = [] if so_far is None else list(so_far)
    return pl.pallas_call(
        functools.partial(green_kernel, at=at, rows=rows),
        in_specs=[SM] + [VM] * (5 + len(carried)),
        out_specs=[VM, VM],
        out_shape=[pltpu.VMEM((4, M, NEL), BF16), pltpu.VMEM((2, M, NEL), BF16)],
        scratch_shapes=[pltpu.VMEM((2, rows, NEL), BF16)],
        input_output_aliases={6: 0, 7: 1} if carried else {},
        compiler_params=pltpu.CompilerParams(vmem_limit_bytes=16 * MIB),
    )(src, own, core, pair, diag, inv, *carried)


def load_blocks(refs):
    found = []
    for ref in refs:
        found += [ref[...]] if len(ref.shape) == 2 else [ref[i] for i in range(ref.shape[0])]
    return found


def count_blocks(arrays):
    return sum(1 if a.ndim == 2 else a.shape[0] for a in arrays)


def pair_products(blocks, green_ref, walkers, rot_ref):
    for l, f in enumerate(blocks):
        for i, w in enumerate(walkers):
            rot_ref[i * NEL : (i + 1) * NEL, l * NEL : (l + 1) * NEL] = dot(f, green_ref[w]).astype(BF16)
    return jnp.concatenate(blocks, axis=0)


def first_kernel(*refs, n):
    f_refs, green_ref, new_ref = refs[:n], refs[n], refs[n + 1]
    out_ref, combed_ref, rot_ref, sem = refs[n + 2 :]
    copy = pltpu.make_async_copy(new_ref, combed_ref.at[:, 0], sem)
    copy.start()
    stacked = pair_products(load_blocks(f_refs), green_ref, range(4), rot_ref)
    for m in range(0, M, NEL):
        out_ref[:, m : m + NEL] = dot(rot_ref[...], stacked[:, m : m + NEL])
    copy.wait()


def first_part(arrays, green, new):
    n, count = len(arrays), count_blocks(arrays)
    return pl.pallas_call(
        functools.partial(first_kernel, n=n),
        in_specs=[VM] * (n + 2),
        out_specs=[VM, pl.BlockSpec(memory_space=pl.ANY)],
        out_shape=[pltpu.VMEM((4 * NEL, M), F32), jax.ShapeDtypeStruct((2, 1, M, NEL), BF16)],
        scratch_shapes=[pltpu.VMEM((4 * NEL, count * NEL), BF16), pltpu.SemaphoreType.DMA],
        compiler_params=pltpu.CompilerParams(vmem_limit_bytes=24 * MIB),
        cost_estimate=pl.CostEstimate(
            flops=count * 16 * NEL * NEL * M, transcendentals=0, bytes_accessed=count * MIB // 2
        ),
    )(*arrays, green, new)


def main_kernel(*refs, n):
    f_refs, green_ref, acc_ref, out_ref, rot_ref = refs[:n], refs[n], refs[n + 1], refs[-2], refs[-1]
    stacked = pair_products(load_blocks(f_refs), green_ref, range(4), rot_ref)
    for m in range(0, M, NEL):
        out_ref[:, m : m + NEL] = acc_ref[:, m : m + NEL] + dot(rot_ref[...], stacked[:, m : m + NEL])


def main_part(arrays, green, running):
    n, count = len(arrays), count_blocks(arrays)
    return pl.pallas_call(
        functools.partial(main_kernel, n=n),
        in_specs=[VM] * (n + 2),
        out_specs=VM,
        out_shape=pltpu.VMEM((4 * NEL, M), F32),
        scratch_shapes=[pltpu.VMEM((4 * NEL, count * NEL), BF16)],
        input_output_aliases={n + 1: 0},
        compiler_params=pltpu.CompilerParams(vmem_limit_bytes=24 * MIB),
        cost_estimate=pl.CostEstimate(
            flops=count * 16 * NEL * NEL * M, transcendentals=0, bytes_accessed=count * MIB // 2
        ),
    )(*arrays, green, running)


def last_kernel(*refs, n, low):
    f_refs, green_ref, acc_ref, out_ref, rot_ref = refs[:n], refs[n], refs[n + 1], refs[-2], refs[-1]
    stacked = pair_products(load_blocks(f_refs), green_ref, (low, low + 1), rot_ref)
    for m in range(0, M, NEL):
        added = dot(rot_ref[...], stacked[:, m : m + NEL])
        total = acc_ref[low * NEL : (low + 2) * NEL, m : m + NEL] + added
        out_ref[:, m : m + NEL] = total.astype(out_ref.dtype)


def last_part(arrays, green, running, low, out_shape):
    n, count = len(arrays), count_blocks(arrays)
    return pl.pallas_call(
        functools.partial(last_kernel, n=n, low=low),
        in_specs=[VM] * (n + 2),
        out_specs=VM,
        out_shape=out_shape,
        scratch_shapes=[pltpu.VMEM((2 * NEL, count * NEL), BF16)],
        compiler_params=pltpu.CompilerParams(vmem_limit_bytes=24 * MIB),
        cost_estimate=pl.CostEstimate(
            flops=count * 8 * NEL * NEL * M, transcendentals=0, bytes_accessed=count * MIB // 2
        ),
    )(*arrays, green, running)


def combine_kernel(own_ref, other_ref, out_ref):
    out_ref[0, 0] = -(own_ref[...] + other_ref[...].astype(F32)).T


def combine(own, other):
    part = pl.BlockSpec((NEL, M), lambda w: (w, 0))
    return pl.pallas_call(
        combine_kernel,
        grid=(2,),
        in_specs=[part, part],
        out_specs=pl.BlockSpec((1, 1, M, NEL), lambda w: (w, 0, 0, 0)),
        out_shape=jax.ShapeDtypeStruct((2, 1, M, NEL), F32),
        compiler_params=pltpu.CompilerParams(vmem_limit_bytes=16 * MIB),
        name="combine",
    )(own, other)


def step(walkers, counts, slot_copy, factors):
    swapped = swap_factor(factors.reshape(NEL, M))
    kind = lax.broadcasted_iota(jnp.int32, (2, 16, NEL), 1)
    info = jnp.where(kind == 0, counts[:, :, None], slot_copy[:, :, None]).astype(BF16)
    top = jnp.concatenate([walkers[:, 0, :NEL], info], axis=1)
    pair_top = to_pair(top)
    core_top = to_core(top)
    rest = walkers[:, 0, NEL:]
    pair_rest = to_pair(rest)
    core_rest = to_core(rest)
    diag_top = to_core(pair_top)
    my = lax.axis_index("walk").astype(jnp.int32).reshape(1)
    src, inv = newton(my, top, core_top, pair_top, diag_top)

    f = {(0, 0): swapped}
    f[-1, 0] = along_a(swapped, 1)
    f[1, 0] = along_a(swapped, -1)
    f[0, -1] = along_b(swapped, 1)
    f[0, 1] = along_b(swapped, -1)
    f[2, 0] = along_a(f[-1, 0], 1)
    sides = jnp.stack([f[-1, 0], f[1, 0]])
    sides_below = along_b(sides, 1)
    sides_above = along_b(sides, -1)
    f[0, 2] = along_b(f[0, 1], -1)
    f[2, -1] = along_b(f[2, 0], 1)
    f[2, 1] = along_b(f[2, 0], -1)
    sides_far = along_b(sides_below, 1)
    f[2, 2] = along_b(f[2, 1], -1)

    part = green_piece(src, top, core_top, pair_top, diag_top, inv, None, 0, NEL)
    diag_rest = to_core(pair_rest)
    green, new = green_piece(src, rest, core_rest, pair_rest, diag_rest, inv, part, NEL, M - NEL)

    running, combed = first_part([f[0, 0], f[-1, 0], f[1, 0], f[0, -1], f[0, 1]], green, new)
    running = main_part([f[2, 0], f[0, 2]], green, running)
    running = main_part([sides_below, sides_above], green, running)
    running = main_part([f[2, -1], f[2, 1]], green, running)
    blocks = [sides_far, f[2, 2]]
    half = (2 * NEL, M)
    other = to_core(last_part(blocks, green, running, 2, jax.ShapeDtypeStruct(half, BF16)))
    own = last_part(blocks, green, running, 0, pltpu.VMEM(half, F32))
    return combed, combine(own, other)


def solution(mesh):
    in_specs = (
        P("walk", "chol", None, None),
        P("walk", "chol"),
        P("walk", "chol"),
        P("chol", None, None),
    )
    out_specs = (P("walk", "chol", None, None), P("walk", "chol", None, None))
    return jax.shard_map(step, mesh=mesh, in_specs=in_specs, out_specs=out_specs, check_vma=False)
```

time: 326 us -> 97 us (0.30)
  waiting for transfers between devices: 187 us -> 25.2 us
  matrix products: 84.2 us -> 0 us
  Pallas kernels: 0 us -> 34.7 us
  starting transfers between devices: 0.08 us -> 30.3 us
  other arithmetic: 25.1 us -> 1.91 us
  between operations: 14.8 us -> 0.83 us
  local copies, waits for them, and re-layouts: 7.37 us -> 2.17 us
  blocking collectives: 5.01 us -> 0 us
    all_gather x2 -> x0, waiting for transfers between devices: 185 us -> none  [the longest x1 146 us: body(): lax.all_gather(factors, 'chol', axis=0, tiled=True)]
    dot_general x49 -> x0, matrix products: 84.2 us -> none  [the longest x32 74 us: shard_term(): jnp.einsum('lam,wlia->wmi', factor_block, rotated, preferred_element_type...]
    pallas_call x0 -> x10, Pallas kernels: none -> 34.7 us  [the longest x3 12.2 us: main_part(): pl.pallas_call(functools.partial(main_kernel, n=n), in_specs=[VM] * (n +...]
    ppermute x0 -> x20, starting transfers between devices: none -> 30.3 us  [moved(): return lax.ppermute(x, ('walk', 'chol'), pairs)]
    ppermute x0 -> x20, waiting for transfers between devices: none -> 25.2 us  [moved(): return lax.ppermute(x, ('walk', 'chol'), pairs)]
    add x32 -> x0, other arithmetic: 21.9 us -> none  [one_shard(): return (partial_value + shard_term(factor_block, green_block), None)]
    unnamed x1 -> x0, blocking collectives: 5.01 us -> none
  transfers between devices with their start and end apart: 2 -> 20, of which waited for: 2 -> 6; matrix products, arithmetic and copies ran while one was open for 6% -> 4% of each run, Pallas kernels for 0% -> 33%
where the time goes in v1:
time: 97 us; the launch traced here: 95.1 us
  Pallas kernels  34.7 us (36%)
  starting transfers between devices  30.3 us (31%)
  waiting for transfers between devices  25.2 us (26%)
  local copies, waits for them, and re-layouts  2.17 us (2%)
  other arithmetic  1.91 us (2%)
    ppermute x20, starting transfers between devices, moved(): return lax.ppermute(x, ('walk', 'chol'), pairs)  30.3 us
    ppermute x20, waiting for transfers between devices, moved(): return lax.ppermute(x, ('walk', 'chol'), pairs)  25.2 us
    pallas_call x3, Pallas kernels, main_part(): pl.pallas_call(functools.partial(main_kernel, n=n), in_specs=[VM] * (n +...  12.2 us
    pallas_call x1, Pallas kernels, newton(): pl.pallas_call(newton_kernel, in_specs=[SM, VM, VM, VM, VM], out_specs=[S...  7.47 us
    pallas_call x1, Pallas kernels, first_part(): pl.pallas_call(functools.partial(first_kernel, n=n), in_specs=[VM] * (n +...  6.95 us
    pallas_call x2, Pallas kernels, last_part(): pl.pallas_call(functools.partial(last_kernel, n=n, low=low), in_specs=[VM...  3.59 us
    pallas_call x2, Pallas kernels, green_piece(): pl.pallas_call(functools.partial(green_kernel, at=at, rows=rows), in_spec...  2.89 us
  transfers between devices with their start and end apart: 20, of which 6 were waited for; matrix products, arithmetic and copies ran while one was open for 4% of the time, Pallas kernels for 33%

profile of v1, /device:TPU:0, one launch (start us, length us, event | category | flops | bytes accessed | tf_op | source)
XLA Modules:
  0.0 95.1 jit_solution(6394860169824983314)
XLA Ops:
  0.6 5.4 %collective-permute-start = (bf16[256,1024]{1,0:T(8,128)(2,1)}, bf16[256,1024]{1,0:T(8,128)(2,1)}, u32[]{:S(2)}, u32[]{:S(2)}) collective-permute-start(bf16[256,1024]{1,0:T(8,128)(2,1)} %bitcast.17), channel_id=1, source_target_pairs={{0,0},{1,96},{2,2},{3,98},{4,4},{5,100},{6,6},{7,102},{8,8},{9,104... | collective-permute-start | bytes 1572872 | tf_op jit(solution)/shard_map/ppermute | solution.py:39
  7.2 1.7 %collective-permute-start.9 = (bf16[2,768,256]{2,1,0:T(8,128)(2,1)S(1)}, bf16[2,768,256]{2,1,0:T(8,128)(2,1)S(1)}, u32[]{:S(2)}, u32[]{:S(2)}) collective-permute-start(bf16[2,768,256]{2,1,0:T(8,128)(2,1)S(1)} %slice_bitcast_fusion.own_ref), channel_id=1, source_target_pairs={{0,64},{1,65},{2,66},{3,67},{4,68},{5,69},{6,70},{7,71},{8,72},{9,... | collective-permute-start | bytes 2359304 | tf_op jit(solution)/shard_map/ppermute | solution.py:39
  8.9 1.6 %collective-permute-start.1 = (bf16[256,1024]{1,0:T(8,128)(2,1)}, bf16[256,1024]{1,0:T(8,128)(2,1)S(1)}, u32[]{:S(2)}, u32[]{:S(2)}) collective-permute-start(bf16[256,1024]{1,0:T(8,128)(2,1)} %collective-permute-done.refs_0_), channel_id=1, source_target_pairs={{0,8},{1,9},{2,10},{3,11},{4,12},{5,13},{6,14},{7,15},{8,16},{9,17... | collective-permute-start | bytes 1572872 | tf_op jit(solution)/shard_map/ppermute | solution.py:39
  10.5 1.7 %collective-permute-start.2 = (bf16[256,1024]{1,0:T(8,128)(2,1)}, bf16[256,1024]{1,0:T(8,128)(2,1)S(1)}, u32[]{:S(2)}, u32[]{:S(2)}) collective-permute-start(bf16[256,1024]{1,0:T(8,128)(2,1)} %collective-permute-done.refs_0_), channel_id=1, source_target_pairs={{0,24},{1,25},{2,26},{3,27},{4,28},{5,29},{6,30},{7,31},{8,0},{9,1... | collective-permute-start | bytes 1572872 | tf_op jit(solution)/shard_map/ppermute | solution.py:39
  14.4 5.1 %collective-permute-done.1.refs_1_ = bf16[256,1024]{1,0:T(8,128)(2,1)S(1)} collective-permute-done((bf16[256,1024]{1,0:T(8,128)(2,1)}, bf16[256,1024]{1,0:T(8,128)(2,1)S(1)}, u32[]{:S(2)}, u32[]{:S(2)}) %collective-permute-start.1) | collective-permute-done | bytes 524320 | tf_op jit(solution)/shard_map/ppermute | solution.py:39
  19.5 3.8 %collective-permute-start.5 = (bf16[2,272,256]{2,1,0:T(8,128)(2,1)S(1)}, bf16[2,272,256]{2,1,0:T(8,128)(2,1)S(1)}, u32[]{:S(2)}, u32[]{:S(2)}) collective-permute-start(bf16[2,272,256]{2,1,0:T(8,128)(2,1)S(1)} %pad_maximum_fusion.1.own_ref), channel_id=1, source_target_pairs={{0,32},{1,33},{2,34},{3,35},{4,36},{5,37},{6,38},{7,39},{8,40},{9,... | collective-permute-start | bytes 835592 | tf_op jit(solution)/shard_map/ppermute | solution.py:39
  24.4 7.8 %collective-permute-done.6.pair_ref = bf16[2,272,256]{2,1,0:T(8,128)(2,1)S(1)} collective-permute-done((bf16[2,272,256]{2,1,0:T(8,128)(2,1)S(1)}, bf16[2,272,256]{2,1,0:T(8,128)(2,1)S(1)}, u32[]{:S(2)}, u32[]{:S(2)}) %collective-permute-start.6) | collective-permute-done | bytes 278560 | tf_op jit(solution)/shard_map/ppermute | solution.py:39
  32.2 4.0 %collective-permute-start.4 = (bf16[256,1024]{1,0:T(8,128)(2,1)}, bf16[256,1024]{1,0:T(8,128)(2,1)}, u32[]{:S(2)}, u32[]{:S(2)}) collective-permute-start(bf16[256,1024]{1,0:T(8,128)(2,1)} %collective-permute-done.refs_0_), channel_id=1, source_target_pairs={{0,6},{1,7},{2,0},{3,1},{4,2},{5,3},{6,4},{7,5},{8,14},{9,15},{10,... | collective-permute-start | bytes 1572872 | tf_op jit(solution)/shard_map/ppermute | solution.py:39
  37.8 1.6 %collective-permute-start.13 = (bf16[256,1024]{1,0:T(8,128)(2,1)S(1)}, bf16[256,1024]{1,0:T(8,128)(2,1)}, u32[]{:S(2)}, u32[]{:S(2)}) collective-permute-start(bf16[256,1024]{1,0:T(8,128)(2,1)S(1)} %collective-permute-done.1.refs_1_), channel_id=1, source_target_pairs={{0,8},{1,9},{2,10},{3,11},{4,12},{5,13},{6,14},{7,15},{8,16},{9,17... | collective-permute-start | bytes 1572872 | tf_op jit(solution)/shard_map/ppermute | solution.py:39
  39.4 3.9 %collective-permute-done.4.refs_4_ = bf16[256,1024]{1,0:T(8,128)(2,1)} collective-permute-done((bf16[256,1024]{1,0:T(8,128)(2,1)}, bf16[256,1024]{1,0:T(8,128)(2,1)}, u32[]{:S(2)}, u32[]{:S(2)}) %collective-permute-start.4) | collective-permute-done | bytes 524320 | tf_op jit(solution)/shard_map/ppermute | solution.py:39
  43.3 3.7 %collective-permute-start.17 = (bf16[2,256,1024]{2,1,0:T(8,128)(2,1)}, bf16[2,256,1024]{2,1,0:T(8,128)(2,1)}, u32[]{:S(2)}, u32[]{:S(2)}) collective-permute-start(bf16[2,256,1024]{2,1,0:T(8,128)(2,1)} %pad_maximum_fusion), channel_id=1, source_target_pairs={{0,6},{1,7},{2,0},{3,1},{4,2},{5,3},{6,4},{7,5},{8,14},{9,15},{10,... | collective-permute-start | bytes 3145736 | tf_op jit(solution)/shard_map/ppermute | solution.py:39
  47.0 6.5 %collective-permute-done.13.refs_0_ = bf16[256,1024]{1,0:T(8,128)(2,1)} collective-permute-done((bf16[256,1024]{1,0:T(8,128)(2,1)S(1)}, bf16[256,1024]{1,0:T(8,128)(2,1)}, u32[]{:S(2)}, u32[]{:S(2)}) %collective-permute-start.13) | collective-permute-done | bytes 524320 | tf_op jit(solution)/shard_map/ppermute | solution.py:39
  53.6 7.5 %newton.1 = (s32[4]{0:T(128)S(1)}, bf16[4,256,256]{2,1,0:T(8,128)(2,1)S(1)}) custom-call(s32[1]{0:T(128)} %bitcast.1.my_ref, bf16[2,272,256]{2,1,0:T(8,128)(2,1)S(1)} %pad_maximum_fusion.1.own_ref, bf16[2,272,256]{2,1,0:T(8,128)(2,1)S(1)} %collective-permute-done.5.core_ref, bf16[2,272,256]{2,1,0:T(8,128)(2,1)S(1)} %collective-permute-done.6.pair_ref, ...), custom_call_target="tpu_custom_call" | custom-call | tf_op jit(solution)/shard_map/newton/pallas_call | solution.py:159
  63.0 1.9 %shard_map.60 = (bf16[4,1024,256]{2,1,0:T(8,128)(2,1)S(1)}, bf16[2,1024,256]{2,1,0:T(8,128)(2,1)S(1)}) custom-call(s32[4]{0:T(128)S(1)} %get-tuple-element.10.src_ref, bf16[2,768,256]{2,1,0:T(8,128)(2,1)S(1)} %slice_bitcast_fusion.own_ref, bf16[2,768,256]{2,1,0:T(8,128)(2,1)S(1)} %collective-permute-done.8.core_ref, ...), custom_call_target="tpu_custom_call", output_to_operand_aliasing={{0}: (6, {}), {1}: (7, {})} | custom-call | tf_op jit(solution)/shard_map/pallas_call | solution.py:197
  64.9 1.3 %collective-permute-start.16 = (bf16[256,1024]{1,0:T(8,128)(2,1)}, bf16[256,1024]{1,0:T(8,128)(2,1)S(1)}, u32[]{:S(2)}, u32[]{:S(2)}) collective-permute-start(bf16[256,1024]{1,0:T(8,128)(2,1)} %collective-permute-done.13.refs_0_), channel_id=1, source_target_pairs={{0,2},{1,3},{2,4},{3,5},{4,6},{5,7},{6,0},{7,1},{8,10},{9,11},{10,... | collective-permute-start | bytes 1572872 | tf_op jit(solution)/shard_map/ppermute | solution.py:39
  66.2 1.9 %collective-permute-start.12 = (bf16[2,256,1024]{2,1,0:T(8,128)(2,1)}, bf16[2,256,1024]{2,1,0:T(8,128)(2,1)S(1)}, u32[]{:S(2)}, u32[]{:S(2)}) collective-permute-start(bf16[2,256,1024]{2,1,0:T(8,128)(2,1)} %collective-permute-done.11.refs_0_), channel_id=1, source_target_pairs={{0,2},{1,3},{2,4},{3,5},{4,6},{5,7},{6,0},{7,1},{8,10},{9,11},{10,... | collective-permute-start | bytes 3145736 | tf_op jit(solution)/shard_map/ppermute | solution.py:39
  68.1 6.9 %shard_map.61 = (f32[1024,1024]{1,0:T(8,128)S(1)}, bf16[2,1,1024,256]{3,2,1,0:T(8,128)(2,1)}) custom-call(bf16[256,1024]{1,0:T(8,128)(2,1)} %collective-permute-done.refs_0_, bf16[256,1024]{1,0:T(8,128)(2,1)S(1)} %copy-done.1, bf16[256,1024]{1,0:T(8,128)(2,1)S(1)} %copy-done.3, bf16[256,1024]{1,0:T(8,128)(2,1)} %collective-permute-done.3.refs_3_, ...), custom_call_target="tpu_custom_call" | custom-call | flops 5368709120 | bytes 2621440 | tf_op jit(solution)/shard_map/pallas_call | solution.py:239
  75.1 3.7 %shard_map.62.refs_3_ = f32[1024,1024]{1,0:T(8,128)S(1)} custom-call(bf16[256,1024]{1,0:T(8,128)(2,1)} %collective-permute-done.13.refs_0_, bf16[256,1024]{1,0:T(8,128)(2,1)} %collective-permute-done.18.refs_1_, bf16[4,1024,256]{2,1,0:T(8,128)(2,1)S(1)} %get-tuple-element.14.refs_5_.refs_2_, ...), custom_call_target="tpu_custom_call", output_to_operand_aliasing={{}: (3, {})} | custom-call | flops 2147483648 | bytes 1048576 | tf_op jit(solution)/shard_map/pallas_call | solution.py:261
  78.7 1.6 %collective-permute-start.15 = (bf16[256,1024]{1,0:T(8,128)(2,1)S(1)}, bf16[256,1024]{1,0:T(8,128)(2,1)S(1)}, u32[]{:S(2)}, u32[]{:S(2)}) collective-permute-start(bf16[256,1024]{1,0:T(8,128)(2,1)S(1)} %collective-permute-done.14.refs_1_), channel_id=1, source_target_pairs={{0,6},{1,7},{2,0},{3,1},{4,2},{5,3},{6,4},{7,5},{8,14},{9,15},{10,... | collective-permute-start | bytes 1572872 | tf_op jit(solution)/shard_map/ppermute | solution.py:39
  80.4 6.1 %shard_map.63.refs_3_ = f32[1024,1024]{1,0:T(8,128)S(1)} custom-call(bf16[2,256,1024]{2,1,0:T(8,128)(2,1)} %collective-permute-done.11.refs_0_, bf16[2,256,1024]{2,1,0:T(8,128)(2,1)} %collective-permute-done.17.refs_1_, bf16[4,1024,256]{2,1,0:T(8,128)(2,1)S(1)} %get-tuple-element.14.refs_5_.refs_2_, ...), custom_call_target="tpu_custom_call", output_to_operand_aliasing={{}: (3, {})} | custom-call | flops 4294967296 | bytes 2097152 | tf_op jit(solution)/shard_map/pallas_call | solution.py:261
  86.5 2.5 %shard_map.64.refs_3_ = f32[1024,1024]{1,0:T(8,128)S(1)} custom-call(bf16[256,1024]{1,0:T(8,128)(2,1)S(1)} %collective-permute-done.16.refs_0_, bf16[256,1024]{1,0:T(8,128)(2,1)S(1)} %collective-permute-done.14.refs_1_, bf16[4,1024,256]{2,1,0:T(8,128)(2,1)S(1)} %get-tuple-element.14.refs_5_.refs_2_, ...), custom_call_target="tpu_custom_call", output_to_operand_aliasing={{}: (3, {})} | custom-call | flops 2147483648 | bytes 1048576 | tf_op jit(solution)/shard_map/pallas_call | solution.py:261
  88.9 1.8 %shard_map.66 = bf16[512,1024]{1,0:T(8,128)(2,1)S(1)} custom-call(bf16[2,256,1024]{2,1,0:T(8,128)(2,1)S(1)} %collective-permute-done.12.refs_0_, bf16[256,1024]{1,0:T(8,128)(2,1)S(1)} %collective-permute-done.15.refs_1_, bf16[4,1024,256]{2,1,0:T(8,128)(2,1)S(1)} %get-tuple-element.14.refs_5_.refs_2_, f32[1024,1024]{1,0:T(8,128)S(1)} %shard_map.64.refs_3_), custom_call_target="tpu_custom_call" | custom-call | flops 1610612736 | bytes 1572864 | tf_op jit(solution)/shard_map/pallas_call | solution.py:286
  90.8 1.8 %shard_map.65.own_ref = f32[512,1024]{1,0:T(8,128)S(1)} custom-call(bf16[2,256,1024]{2,1,0:T(8,128)(2,1)S(1)} %collective-permute-done.12.refs_0_, bf16[256,1024]{1,0:T(8,128)(2,1)S(1)} %collective-permute-done.15.refs_1_, bf16[4,1024,256]{2,1,0:T(8,128)(2,1)S(1)} %get-tuple-element.14.refs_5_.refs_2_, f32[1024,1024]{1,0:T(8,128)S(1)} %shard_map.64.refs_3_), custom_call_target="tpu_custom_call" | custom-call | flops 1610612736 | bytes 1572864 | tf_op jit(solution)/shard_map/pallas_call | solution.py:286
  93.5 1.7 %combine.1 = f32[2,1,1024,256]{3,2,1,0:T(8,128)} custom-call(f32[512,1024]{1,0:T(8,128)S(1)} %shard_map.65.own_ref, bf16[512,1024]{1,0:T(8,128)(2,1)S(1)} %collective-permute-done.19.other_ref), custom_call_target="tpu_custom_call" | custom-call | tf_op jit(solution)/shard_map/combine/pallas_call | solution.py:305
  (40 shorter events, 9.1 us)
Async XLA Ops:
  0.6 8.2 %collective-permute-start = (bf16[256,1024]{1,0:T(8,128)(2,1)}, bf16[256,1024]{1,0:T(8,128)(2,1)}, u32[]{:S(2)}, u32[]{:S(2)}) collective-permute-start(bf16[256,1024]{1,0:T(8,128)(2,1)} %bitcast.17), channel_id=1, source_target_pairs={{0,0},{1,96},{2,2},{3,98},{4,4},{5,100},{6,6},{7,102},{8,8},{9,104... | collective-permute-start | bytes 1572872 | tf_op jit(solution)/shard_map/ppermute | solution.py:39
  7.2 29.1 %collective-permute-start.9 = (bf16[2,768,256]{2,1,0:T(8,128)(2,1)S(1)}, bf16[2,768,256]{2,1,0:T(8,128)(2,1)S(1)}, u32[]{:S(2)}, u32[]{:S(2)}) collective-permute-start(bf16[2,768,256]{2,1,0:T(8,128)(2,1)S(1)} %slice_bitcast_fusion.own_ref), channel_id=1, source_target_pairs={{0,64},{1,65},{2,66},{3,67},{4,68},{5,69},{6,70},{7,71},{8,72},{9,... | collective-permute-start | bytes 2359304 | tf_op jit(solution)/shard_map/ppermute | solution.py:39
  8.9 30.5 %collective-permute-start.8 = (bf16[2,768,256]{2,1,0:T(8,128)(2,1)S(1)}, bf16[2,768,256]{2,1,0:T(8,128)(2,1)S(1)}, u32[]{:S(2)}, u32[]{:S(2)}) collective-permute-start(bf16[2,768,256]{2,1,0:T(8,128)(2,1)S(1)} %slice_bitcast_fusion.own_ref), channel_id=1, source_target_pairs={{0,32},{1,33},{2,34},{3,35},{4,36},{5,37},{6,38},{7,39},{8,40},{9,... | collective-permute-start | bytes 2359304 | tf_op jit(solution)/shard_map/ppermute | solution.py:39
  8.9 10.6 %collective-permute-start.1 = (bf16[256,1024]{1,0:T(8,128)(2,1)}, bf16[256,1024]{1,0:T(8,128)(2,1)S(1)}, u32[]{:S(2)}, u32[]{:S(2)}) collective-permute-start(bf16[256,1024]{1,0:T(8,128)(2,1)} %collective-permute-done.refs_0_), channel_id=1, source_target_pairs={{0,8},{1,9},{2,10},{3,11},{4,12},{5,13},{6,14},{7,15},{8,16},{9,17... | collective-permute-start | bytes 1572872 | tf_op jit(solution)/shard_map/ppermute | solution.py:39
  10.5 12.8 %collective-permute-start.2 = (bf16[256,1024]{1,0:T(8,128)(2,1)}, bf16[256,1024]{1,0:T(8,128)(2,1)S(1)}, u32[]{:S(2)}, u32[]{:S(2)}) collective-permute-start(bf16[256,1024]{1,0:T(8,128)(2,1)} %collective-permute-done.refs_0_), channel_id=1, source_target_pairs={{0,24},{1,25},{2,26},{3,27},{4,28},{5,29},{6,30},{7,31},{8,0},{9,1... | collective-permute-start | bytes 1572872 | tf_op jit(solution)/shard_map/ppermute | solution.py:39
  13.9 18.4 %collective-permute-start.6 = (bf16[2,272,256]{2,1,0:T(8,128)(2,1)S(1)}, bf16[2,272,256]{2,1,0:T(8,128)(2,1)S(1)}, u32[]{:S(2)}, u32[]{:S(2)}) collective-permute-start(bf16[2,272,256]{2,1,0:T(8,128)(2,1)S(1)} %pad_maximum_fusion.1.own_ref), channel_id=1, source_target_pairs={{0,64},{1,65},{2,66},{3,67},{4,68},{5,69},{6,70},{7,71},{8,72},{9,... | collective-permute-start | bytes 835592 | tf_op jit(solution)/shard_map/ppermute | solution.py:39
  19.5 19.9 %copy-start = (bf16[256,1024]{1,0:T(8,128)(2,1)}, bf16[256,1024]{1,0:T(8,128)(2,1)S(1)}, u32[]{:S(2)}) copy-start(bf16[256,1024]{1,0:T(8,128)(2,1)S(1)} %collective-permute-done.1.refs_1_) | copy-start | bytes 1572868
  19.5 16.8 %collective-permute-start.5 = (bf16[2,272,256]{2,1,0:T(8,128)(2,1)S(1)}, bf16[2,272,256]{2,1,0:T(8,128)(2,1)S(1)}, u32[]{:S(2)}, u32[]{:S(2)}) collective-permute-start(bf16[2,272,256]{2,1,0:T(8,128)(2,1)S(1)} %pad_maximum_fusion.1.own_ref), channel_id=1, source_target_pairs={{0,32},{1,33},{2,34},{3,35},{4,36},{5,37},{6,38},{7,39},{8,40},{9,... | collective-permute-start | bytes 835592 | tf_op jit(solution)/shard_map/ppermute | solution.py:39
  23.2 30.2 %copy-start.2 = (bf16[256,1024]{1,0:T(8,128)(2,1)}, bf16[256,1024]{1,0:T(8,128)(2,1)S(1)}, u32[]{:S(2)}) copy-start(bf16[256,1024]{1,0:T(8,128)(2,1)S(1)} %collective-permute-done.2.refs_2_) | copy-start | bytes 1572868
  24.4 41.8 %collective-permute-start.11 = (bf16[2,256,1024]{2,1,0:T(8,128)(2,1)}, bf16[2,256,1024]{2,1,0:T(8,128)(2,1)}, u32[]{:S(2)}, u32[]{:S(2)}) collective-permute-start(bf16[2,256,1024]{2,1,0:T(8,128)(2,1)} %pad_maximum_fusion), channel_id=1, source_target_pairs={{0,2},{1,3},{2,4},{3,5},{4,6},{5,7},{6,0},{7,1},{8,10},{9,11},{10,... | collective-permute-start | bytes 3145736 | tf_op jit(solution)/shard_map/ppermute | solution.py:39
  32.2 11.1 %collective-permute-start.4 = (bf16[256,1024]{1,0:T(8,128)(2,1)}, bf16[256,1024]{1,0:T(8,128)(2,1)}, u32[]{:S(2)}, u32[]{:S(2)}) collective-permute-start(bf16[256,1024]{1,0:T(8,128)(2,1)} %collective-permute-done.refs_0_), channel_id=1, source_target_pairs={{0,6},{1,7},{2,0},{3,1},{4,2},{5,3},{6,4},{7,5},{8,14},{9,15},{10,... | collective-permute-start | bytes 1572872 | tf_op jit(solution)/shard_map/ppermute | solution.py:39
  36.3 1.6 %collective-permute-start.7 = (bf16[2,272,256]{2,1,0:T(8,128)(2,1)S(1)}, bf16[2,272,256]{2,1,0:T(8,128)(2,1)S(1)}, u32[]{:S(2)}, u32[]{:S(2)}) collective-permute-start(bf16[2,272,256]{2,1,0:T(8,128)(2,1)S(1)} %collective-permute-done.6.pair_ref), channel_id=1, source_target_pairs={{0,32},{1,33},{2,34},{3,35},{4,36},{5,37},{6,38},{7,39},{8,40},{9,... | collective-permute-start | bytes 835592 | tf_op jit(solution)/shard_map/ppermute | solution.py:39
  36.3 25.8 %collective-permute-start.10 = (bf16[2,768,256]{2,1,0:T(8,128)(2,1)S(1)}, bf16[2,768,256]{2,1,0:T(8,128)(2,1)}, u32[]{:S(2)}, u32[]{:S(2)}) collective-permute-start(bf16[2,768,256]{2,1,0:T(8,128)(2,1)S(1)} %collective-permute-done.9.pair_ref), channel_id=1, source_target_pairs={{0,32},{1,33},{2,34},{3,35},{4,36},{5,37},{6,38},{7,39},{8,40},{9,... | collective-permute-start | bytes 2359304 | tf_op jit(solution)/shard_map/ppermute | solution.py:39
  37.8 15.6 %collective-permute-start.13 = (bf16[256,1024]{1,0:T(8,128)(2,1)S(1)}, bf16[256,1024]{1,0:T(8,128)(2,1)}, u32[]{:S(2)}, u32[]{:S(2)}) collective-permute-start(bf16[256,1024]{1,0:T(8,128)(2,1)S(1)} %collective-permute-done.1.refs_1_), channel_id=1, source_target_pairs={{0,8},{1,9},{2,10},{3,11},{4,12},{5,13},{6,14},{7,15},{8,16},{9,17... | collective-permute-start | bytes 1572872 | tf_op jit(solution)/shard_map/ppermute | solution.py:39
  39.4 25.5 %collective-permute-start.3 = (bf16[256,1024]{1,0:T(8,128)(2,1)}, bf16[256,1024]{1,0:T(8,128)(2,1)}, u32[]{:S(2)}, u32[]{:S(2)}) collective-permute-start(bf16[256,1024]{1,0:T(8,128)(2,1)} %collective-permute-done.refs_0_), channel_id=1, source_target_pairs={{0,2},{1,3},{2,4},{3,5},{4,6},{5,7},{6,0},{7,1},{8,10},{9,11},{10,... | collective-permute-start | bytes 1572872 | tf_op jit(solution)/shard_map/ppermute | solution.py:39
  43.3 37.1 %collective-permute-start.17 = (bf16[2,256,1024]{2,1,0:T(8,128)(2,1)}, bf16[2,256,1024]{2,1,0:T(8,128)(2,1)}, u32[]{:S(2)}, u32[]{:S(2)}) collective-permute-start(bf16[2,256,1024]{2,1,0:T(8,128)(2,1)} %pad_maximum_fusion), channel_id=1, source_target_pairs={{0,6},{1,7},{2,0},{3,1},{4,2},{5,3},{6,4},{7,5},{8,14},{9,15},{10,... | collective-permute-start | bytes 3145736 | tf_op jit(solution)/shard_map/ppermute | solution.py:39
  53.5 21.6 %collective-permute-start.18 = (bf16[256,1024]{1,0:T(8,128)(2,1)}, bf16[256,1024]{1,0:T(8,128)(2,1)}, u32[]{:S(2)}, u32[]{:S(2)}) collective-permute-start(bf16[256,1024]{1,0:T(8,128)(2,1)} %collective-permute-done.4.refs_4_), channel_id=1, source_target_pairs={{0,6},{1,7},{2,0},{3,1},{4,2},{5,3},{6,4},{7,5},{8,14},{9,15},{10,... | collective-permute-start | bytes 1572872 | tf_op jit(solution)/shard_map/ppermute | solution.py:39
  61.1 7.0 %copy-start.1 = (bf16[256,1024]{1,0:T(8,128)(2,1)S(1)}, bf16[256,1024]{1,0:T(8,128)(2,1)}, u32[]{:S(2)}) copy-start(bf16[256,1024]{1,0:T(8,128)(2,1)} %copy-done) | copy-start | bytes 1572868
  61.1 7.0 %copy-start.3 = (bf16[256,1024]{1,0:T(8,128)(2,1)S(1)}, bf16[256,1024]{1,0:T(8,128)(2,1)}, u32[]{:S(2)}) copy-start(bf16[256,1024]{1,0:T(8,128)(2,1)} %copy-done.2) | copy-start | bytes 1572868
  62.1 16.6 %collective-permute-start.14 = (bf16[256,1024]{1,0:T(8,128)(2,1)}, bf16[256,1024]{1,0:T(8,128)(2,1)S(1)}, u32[]{:S(2)}, u32[]{:S(2)}) collective-permute-start(bf16[256,1024]{1,0:T(8,128)(2,1)} %collective-permute-done.13.refs_0_), channel_id=1, source_target_pairs={{0,6},{1,7},{2,0},{3,1},{4,2},{5,3},{6,4},{7,5},{8,14},{9,15},{10,... | collective-permute-start | bytes 1572872 | tf_op jit(solution)/shard_map/ppermute | solution.py:39
  64.9 21.5 %collective-permute-start.16 = (bf16[256,1024]{1,0:T(8,128)(2,1)}, bf16[256,1024]{1,0:T(8,128)(2,1)S(1)}, u32[]{:S(2)}, u32[]{:S(2)}) collective-permute-start(bf16[256,1024]{1,0:T(8,128)(2,1)} %collective-permute-done.13.refs_0_), channel_id=1, source_target_pairs={{0,2},{1,3},{2,4},{3,5},{4,6},{5,7},{6,0},{7,1},{8,10},{9,11},{10,... | collective-permute-start | bytes 1572872 | tf_op jit(solution)/shard_map/ppermute | solution.py:39
  66.2 22.7 %collective-permute-start.12 = (bf16[2,256,1024]{2,1,0:T(8,128)(2,1)}, bf16[2,256,1024]{2,1,0:T(8,128)(2,1)S(1)}, u32[]{:S(2)}, u32[]{:S(2)}) collective-permute-start(bf16[2,256,1024]{2,1,0:T(8,128)(2,1)} %collective-permute-done.11.refs_0_), channel_id=1, source_target_pairs={{0,2},{1,3},{2,4},{3,5},{4,6},{5,7},{6,0},{7,1},{8,10},{9,11},{10,... | collective-permute-start | bytes 3145736 | tf_op jit(solution)/shard_map/ppermute | solution.py:39
  78.7 10.2 %collective-permute-start.15 = (bf16[256,1024]{1,0:T(8,128)(2,1)S(1)}, bf16[256,1024]{1,0:T(8,128)(2,1)S(1)}, u32[]{:S(2)}, u32[]{:S(2)}) collective-permute-start(bf16[256,1024]{1,0:T(8,128)(2,1)S(1)} %collective-permute-done.14.refs_1_), channel_id=1, source_target_pairs={{0,6},{1,7},{2,0},{3,1},{4,2},{5,3},{6,4},{7,5},{8,14},{9,15},{10,... | collective-permute-start | bytes 1572872 | tf_op jit(solution)/shard_map/ppermute | solution.py:39
  90.7 2.7 %collective-permute-start.19 = (bf16[512,1024]{1,0:T(8,128)(2,1)S(1)}, bf16[512,1024]{1,0:T(8,128)(2,1)S(1)}, u32[]{:S(2)}, u32[]{:S(2)}) collective-permute-start(bf16[512,1024]{1,0:T(8,128)(2,1)S(1)} %shard_map.66), channel_id=1, source_target_pairs={{0,32},{1,33},{2,34},{3,35},{4,36},{5,37},{6,38},{7,39},{8,40},{9,... | collective-permute-start | bytes 3145736 | tf_op jit(solution)/shard_map/ppermute | solution.py:39

commit v2 on v1

--- a/solution.py
+++ b/solution.py
@@ -17,6 +17,7 @@
 F32 = jnp.float32
 VM = pl.BlockSpec(memory_space=pltpu.VMEM)
 SM = pl.BlockSpec(memory_space=pltpu.SMEM)
+HBM = pl.BlockSpec(memory_space=pltpu.HBM)
 
 
 def dot(a, b):
@@ -35,7 +36,9 @@
                 for z in range(4):
                     for x_hi in range(2):
                         here = (x_lo, core, y, z, x_hi)
-                        pairs.append((line(*here), line(*where(*here))))
+                        there = where(*here)
+                        if there is not None:
+                            pairs.append((line(*here), line(*there)))
     return lax.ppermute(x, ("walk", "chol"), pairs)
 
 
@@ -49,23 +52,31 @@
 
 def swap_factor(x):
     def where(xl, c, y, z, xh):
-        return (xl, c, y, z, xh) if c == xh else (1 - xl, 1 - c, y, z, 1 - xh)
+        return None if c == xh else (1 - xl, 1 - c, y, z, 1 - xh)
 
     return moved(x, where)
 
 
-def along_a(x, s):
+def shifted(core, y, z, along, s):
+    on_y = (core == 0) == (along == "a")
+    return ((y + s) % 4, z) if on_y else (y, (z + s) % 4)
+
+
+def first_along(x, along, s):
     def where(xl, c, y, z, xh):
-        return (xl, c, (y + s) % 4, z, xh) if c == 0 else (xl, c, y, (z + s) % 4, xh)
+        if c == xh:
+            return (xl, c, *shifted(c, y, z, along, s), xh)
+        return (1 - xl, 1 - c, *shifted(1 - c, y, z, along, s), 1 - xh)
 
     return moved(x, where)
 
 
 def along_b(x, s):
-    def where(xl, c, y, z, xh):
-        return (xl, c, y, (z + s) % 4, xh) if c == 0 else (xl, c, (y + s) % 4, z, xh)
-
-    return moved(x, where)
+    return moved(x, lambda xl, c, y, z, xh: (xl, c, *shifted(c, y, z, "b", s), xh))
+
+
+def held(x):
+    return pltpu.with_memory_space_constraint(x, pltpu.HBM)
 
 
 def pick(source, refs, store):
@@ -74,6 +85,87 @@
         @pl.when((source >> 1) == j)
         def _():
             store(ref, source & 1)
+
+
+def pack_kernel(walkers_ref, counts_ref, slots_ref, top_ref, rest_ref, small_ref, sems):
+    copies = [
+        pltpu.make_async_copy(counts_ref, small_ref.at[0], sems.at[2]),
+        pltpu.make_async_copy(slots_ref, small_ref.at[1], sems.at[3]),
+        pltpu.make_async_copy(walkers_ref.at[:, 0, 0:NEL], top_ref.at[:, 0:NEL], sems.at[0]),
+        pltpu.make_async_copy(walkers_ref.at[:, 0, NEL:M], rest_ref, sems.at[1]),
+    ]
+    for copy in copies:
+        copy.start()
+    copies[0].wait()
+    copies[1].wait()
+    row = lax.broadcasted_iota(jnp.int32, (16, NEL), 0)
+    for i in range(2):
+        values = jnp.where(row == 0, small_ref[0, i], small_ref[1, i])
+        top_ref[i, NEL : NEL + 16] = values.astype(F32).astype(BF16)
+    copies[2].wait()
+    copies[3].wait()
+
+
+def pack(walkers, counts, slots):
+    return pl.pallas_call(
+        pack_kernel,
+        in_specs=[HBM, HBM, HBM],
+        out_specs=[VM, VM],
+        out_shape=[pltpu.VMEM((2, NEL + 16, NEL), BF16), pltpu.VMEM((2, M - NEL, NEL), BF16)],
+        scratch_shapes=[pltpu.SMEM((2, 2), jnp.int32), pltpu.SemaphoreType.DMA((4,))],
+        compiler_params=pltpu.CompilerParams(vmem_limit_bytes=4 * MIB),
+        name="pack",
+    )(held(walkers), held(counts[:, 0]), held(slots[:, 0]))
+
+
+def own_kernel(local_ref, kept_ref, swapped_ref, out_ref, sem):
+    @pl.when(local_ref[0] == 1)
+    def _():
+        copy = pltpu.make_async_copy(kept_ref, out_ref, sem)
+        copy.start()
+        copy.wait()
+
+    @pl.when(local_ref[0] != 1)
+    def _():
+        copy = pltpu.make_async_copy(swapped_ref, out_ref, sem)
+        copy.start()
+        copy.wait()
+
+
+def own_factor(local, kept, swapped):
+    return pl.pallas_call(
+        own_kernel,
+        in_specs=[SM, HBM, HBM],
+        out_specs=VM,
+        out_shape=pltpu.VMEM(kept.shape, BF16),
+        scratch_shapes=[pltpu.SemaphoreType.DMA],
+        compiler_params=pltpu.CompilerParams(vmem_limit_bytes=2 * MIB),
+        name="own",
+    )(local, held(kept), held(swapped))
+
+
+def stack_kernel(a_ref, b_ref, out_ref, sems):
+    copies = [
+        pltpu.make_async_copy(a_ref, out_ref.at[0], sems.at[0]),
+        pltpu.make_async_copy(b_ref, out_ref.at[1], sems.at[1]),
+    ]
+    for copy in copies:
+        copy.start()
+    for copy in copies:
+        copy.wait()
+
+
+def stack(a, b):
+    whole = pl.BlockSpec(memory_space=pl.ANY)
+    return pl.pallas_call(
+        stack_kernel,
+        in_specs=[whole, whole],
+        out_specs=VM,
+        out_shape=pltpu.VMEM((2,) + a.shape, BF16),
+        scratch_shapes=[pltpu.SemaphoreType.DMA((2,))],
+        compiler_params=pltpu.CompilerParams(vmem_limit_bytes=4 * MIB),
+        name="stack",
+    )(a, b)
 
 
 def find_sources(my, refs, src_ref):
@@ -99,7 +191,30 @@
     return found
 
 
-def newton_kernel(my_ref, own_ref, core_ref, pair_ref, diag_ref, src_ref, inv_ref, a_ref, x_ref, r_ref, z_ref):
+def split(z_ref, value, high, low):
+    upper = value.astype(BF16)
+    z_ref[high] = upper
+    z_ref[low] = (value - upper.astype(F32)).astype(BF16)
+
+
+def square(x_ref, r_ref, z_ref, last=False):
+    for s in range(4):
+        split(z_ref, x_ref[s], 4 * s, 4 * s + 2)
+        split(z_ref, r_ref[s], 4 * s + 1, 4 * s + 3)
+    for s in range(4):
+        rows = 3 if last else 4
+        both = z_ref[4 * s : 4 * s + rows].reshape(rows * NEL, NEL)
+        by_high = dot(both, z_ref[4 * s + 1])
+        if last:
+            by_low = dot(z_ref[4 * s], z_ref[4 * s + 3])
+            r_ref[s] = by_high[NEL : 2 * NEL]
+        else:
+            by_low = dot(both[: 2 * NEL], z_ref[4 * s + 3])
+            r_ref[s] = by_high[NEL : 2 * NEL] + (by_high[3 * NEL :] + by_low[NEL:])
+        x_ref[s] = x_ref[s] + (by_high[:NEL] + (by_high[2 * NEL : 3 * NEL] + by_low[:NEL]))
+
+
+def newton_kernel(my_ref, own_ref, core_ref, pair_ref, diag_ref, src_ref, new_ref, c_ref, x_ref, r_ref, z_ref):
     refs = (own_ref, core_ref, pair_ref, diag_ref)
     found = find_sources(my_ref[0], refs, src_ref)
     row = lax.broadcasted_iota(jnp.int32, (NEL, NEL), 0)
@@ -108,71 +223,78 @@
     for s in range(4):
 
         def store(ref, i, s=s):
-            a_ref[s] = ref[i, 0:NEL]
+            if s < 2:
+                new_ref[s, 0:NEL] = ref[i, 0:NEL]
+            else:
+                c_ref[s - 2] = ref[i, 0:NEL]
 
         pick(found[s], refs, store)
-
-    def split(value, high, low):
-        upper = value.astype(BF16)
-        z_ref[high] = upper
-        z_ref[low] = (value - upper.astype(F32)).astype(BF16)
-
-    def blocks(s):
-        at = s * 4
-        return at, at + 1, at + 2, at + 3
-
-    for s in range(4):
-        xh, rh, xl, rl = blocks(s)
-        residual = one - a_ref[s].astype(F32)
-        split(residual, rh, rl)
+    for s in range(4):
+        a = new_ref[s, 0:NEL] if s < 2 else c_ref[s - 2]
+        residual = one - a.astype(F32)
+        split(z_ref, residual, 4 * s + 1, 4 * s + 3)
         x_ref[s] = one + residual
     for s in range(4):
-        xh, rh, xl, rl = blocks(s)
-        r_ref[s] = dot(z_ref[rh], z_ref[rh]) + (dot(z_ref[rh], z_ref[rl]) + dot(z_ref[rl], z_ref[rh]))
+        high, low = z_ref[4 * s + 1], z_ref[4 * s + 3]
+        r_ref[s] = dot(high, high) + (dot(high, low) + dot(low, high))
 
     def step(k, carry):
-        for s in range(4):
-            xh, rh, xl, rl = blocks(s)
-            split(x_ref[s], xh, xl)
-            split(r_ref[s], rh, rl)
-        for s in range(4):
-            xh, rh, xl, rl = blocks(s)
-            both = z_ref[xh : xh + 4].reshape(4 * NEL, NEL)
-            by_high = dot(both, z_ref[rh])
-            by_low = dot(both[: 2 * NEL], z_ref[rl])
-            x_ref[s] = x_ref[s] + (by_high[:NEL] + (by_high[2 * NEL : 3 * NEL] + by_low[:NEL]))
-            r_ref[s] = by_high[NEL : 2 * NEL] + (by_high[3 * NEL :] + by_low[NEL:])
+        square(x_ref, r_ref, z_ref)
         return carry
 
-    lax.fori_loop(0, NEWTON - 2, step, 0)
-    for s in range(4):
-        xh, rh, xl, rl = blocks(s)
-        split(x_ref[s], xh, xl)
-        split(r_ref[s], rh, rl)
-    for s in range(4):
-        xh, rh, xl, rl = blocks(s)
-        last = dot(z_ref[xh], z_ref[rh]) + (dot(z_ref[xh], z_ref[rl]) + dot(z_ref[xl], z_ref[rh]))
-        inv_ref[s] = (x_ref[s] + last).astype(BF16)
+    lax.fori_loop(0, NEWTON - 5, step, 0)
 
 
 def newton(my, own, core, pair, diag):
     return pl.pallas_call(
         newton_kernel,
         in_specs=[SM, VM, VM, VM, VM],
-        out_specs=[SM, VM],
+        out_specs=[SM] + [VM] * 4,
         out_shape=[
             jax.ShapeDtypeStruct((4,), jnp.int32),
-            pltpu.VMEM((4, NEL, NEL), BF16),
+            pltpu.VMEM((2, M, NEL), BF16),
+            pltpu.VMEM((2, NEL, NEL), BF16),
+            pltpu.VMEM((4, NEL, NEL), F32),
+            pltpu.VMEM((4, NEL, NEL), F32),
         ],
+        scratch_shapes=[pltpu.VMEM((16, NEL, NEL), BF16)],
+        compiler_params=pltpu.CompilerParams(vmem_limit_bytes=16 * MIB),
+        name="newton",
+    )(my, own, core, pair, diag)
+
+
+def inverse_kernel(x_in_ref, r_in_ref, new_ref, c_ref, inv_ref, green_ref, x_ref, r_ref, z_ref):
+    x_ref[...] = x_in_ref[...]
+    r_ref[...] = r_in_ref[...]
+
+    def step(k, carry):
+        square(x_ref, r_ref, z_ref)
+        return carry
+
+    lax.fori_loop(0, 2, step, 0)
+    square(x_ref, r_ref, z_ref, last=True)
+    for s in range(4):
+        x = x_ref[s]
+        inv = (x + dot(x.astype(BF16), r_ref[s].astype(BF16))).astype(BF16)
+        inv_ref[s] = inv
+        a = new_ref[s, 0:NEL] if s < 2 else c_ref[s - 2]
+        green_ref[s, 0:NEL] = dot(a, inv).astype(BF16)
+
+
+def inverse(x, r, new, c):
+    return pl.pallas_call(
+        inverse_kernel,
+        in_specs=[VM] * 4,
+        out_specs=[VM, VM],
+        out_shape=[pltpu.VMEM((4, NEL, NEL), BF16), pltpu.VMEM((4, M, NEL), BF16)],
         scratch_shapes=[
-            pltpu.VMEM((4, NEL, NEL), BF16),
             pltpu.VMEM((4, NEL, NEL), F32),
             pltpu.VMEM((4, NEL, NEL), F32),
             pltpu.VMEM((16, NEL, NEL), BF16),
         ],
         compiler_params=pltpu.CompilerParams(vmem_limit_bytes=16 * MIB),
-        name="newton",
-    )(my, own, core, pair, diag)
+        name="inverse",
+    )(x, r, new, c)
 
 
 def green_kernel(src_ref, own_ref, core_ref, pair_ref, diag_ref, inv_ref, *rest, at, rows):
@@ -193,14 +315,14 @@
 
 
 def green_piece(src, own, core, pair, diag, inv, so_far, at, rows):
-    carried = [] if so_far is None else list(so_far)
+    carried = list(so_far)
     return pl.pallas_call(
         functools.partial(green_kernel, at=at, rows=rows),
         in_specs=[SM] + [VM] * (5 + len(carried)),
         out_specs=[VM, VM],
         out_shape=[pltpu.VMEM((4, M, NEL), BF16), pltpu.VMEM((2, M, NEL), BF16)],
         scratch_shapes=[pltpu.VMEM((2, rows, NEL), BF16)],
-        input_output_aliases={6: 0, 7: 1} if carried else {},
+        input_output_aliases={6: 0, 7: 1},
         compiler_params=pltpu.CompilerParams(vmem_limit_bytes=16 * MIB),
     )(src, own, core, pair, diag, inv, *carried)
 
@@ -314,26 +436,26 @@
 
 
 def step(walkers, counts, slot_copy, factors):
-    swapped = swap_factor(factors.reshape(NEL, M))
-    kind = lax.broadcasted_iota(jnp.int32, (2, 16, NEL), 1)
-    info = jnp.where(kind == 0, counts[:, :, None], slot_copy[:, :, None]).astype(BF16)
-    top = jnp.concatenate([walkers[:, 0, :NEL], info], axis=1)
+    walk, chol = lax.axis_index("walk").astype(jnp.int32), lax.axis_index("chol").astype(jnp.int32)
+    kept = factors.reshape(NEL, M)
+    local = jnp.where((walk & 1) == (chol & 1), 1, 0).astype(jnp.int32).reshape(1)
+    swapped = own_factor(local, kept, swap_factor(kept))
+    top, rest = pack(walkers, counts, slot_copy)
     pair_top = to_pair(top)
     core_top = to_core(top)
-    rest = walkers[:, 0, NEL:]
     pair_rest = to_pair(rest)
     core_rest = to_core(rest)
     diag_top = to_core(pair_top)
-    my = lax.axis_index("walk").astype(jnp.int32).reshape(1)
-    src, inv = newton(my, top, core_top, pair_top, diag_top)
+    src, new, other_top, x, r = newton(walk.reshape(1), top, core_top, pair_top, diag_top)
+    inv, green = inverse(x, r, new, other_top)
 
     f = {(0, 0): swapped}
-    f[-1, 0] = along_a(swapped, 1)
-    f[1, 0] = along_a(swapped, -1)
+    f[-1, 0] = first_along(kept, "a", 1)
+    f[1, 0] = first_along(kept, "a", -1)
     f[0, -1] = along_b(swapped, 1)
     f[0, 1] = along_b(swapped, -1)
-    f[2, 0] = along_a(f[-1, 0], 1)
-    sides = jnp.stack([f[-1, 0], f[1, 0]])
+    f[2, 0] = moved(swapped, lambda xl, c, y, z, xh: (xl, c, *shifted(c, y, z, "a", 2), xh))
+    sides = stack(f[-1, 0], f[1, 0])
     sides_below = along_b(sides, 1)
     sides_above = along_b(sides, -1)
     f[0, 2] = along_b(f[0, 1], -1)
@@ -342,15 +464,14 @@
     sides_far = along_b(sides_below, 1)
     f[2, 2] = along_b(f[2, 1], -1)
 
-    part = green_piece(src, top, core_top, pair_top, diag_top, inv, None, 0, NEL)
     diag_rest = to_core(pair_rest)
-    green, new = green_piece(src, rest, core_rest, pair_rest, diag_rest, inv, part, NEL, M - NEL)
-
-    running, combed = first_part([f[0, 0], f[-1, 0], f[1, 0], f[0, -1], f[0, 1]], green, new)
-    running = main_part([f[2, 0], f[0, 2]], green, running)
+    green, new = green_piece(src, rest, core_rest, pair_rest, diag_rest, inv, (green, new), NEL, M - NEL)
+
+    running, combed = first_part([f[0, 0], sides], green, new)
+    running = main_part([f[2, 0], f[0, -1], f[0, 1]], green, running)
     running = main_part([sides_below, sides_above], green, running)
     running = main_part([f[2, -1], f[2, 1]], green, running)
-    blocks = [sides_far, f[2, 2]]
+    blocks = [f[0, 2], sides_far, f[2, 2]]
     half = (2 * NEL, M)
     other = to_core(last_part(blocks, green, running, 2, jax.ShapeDtypeStruct(half, BF16)))
     own = last_part(blocks, green, running, 0, pltpu.VMEM(half, F32))

time: 97 us -> 90.8 us (0.936)
  the two profiles are of different devices: /device:TPU:0 before, /device:TPU:13 now
where the time goes in v2:
time: 90.8 us; the launch traced here: 90.5 us
  starting transfers between devices  40.2 us (44%)
  Pallas kernels  35.3 us (39%)
  waiting for transfers between devices  14.1 us (16%)
    ppermute x20, starting transfers between devices, moved(): return lax.ppermute(x, ('walk', 'chol'), pairs)  40.2 us
    ppermute x20, waiting for transfers between devices, moved(): return lax.ppermute(x, ('walk', 'chol'), pairs)  14.1 us
    pallas_call x3, Pallas kernels, main_part(): pl.pallas_call(functools.partial(main_kernel, n=n), in_specs=[VM] * (n +...  11.7 us
    pallas_call x1, Pallas kernels, newton(): pl.pallas_call(newton_kernel, in_specs=[SM, VM, VM, VM, VM], out_specs=[S...  5.32 us
    pallas_call x2, Pallas kernels, last_part(): pl.pallas_call(functools.partial(last_kernel, n=n, low=low), in_specs=[VM...  4.67 us
    pallas_call x1, Pallas kernels, first_part(): pl.pallas_call(functools.partial(first_kernel, n=n), in_specs=[VM] * (n +...  3.43 us
    pallas_call x1, Pallas kernels, inverse(): pl.pallas_call(inverse_kernel, in_specs=[VM] * 4, out_specs=[VM, VM], out...  3.36 us
    pallas_call x1, Pallas kernels, green_piece(): pl.pallas_call(functools.partial(green_kernel, at=at, rows=rows), in_spec...  2.09 us
  transfers between devices with their start and end apart: 20, of which 5 were waited for; matrix products, arithmetic and copies ran while one was open for 0% of the time, Pallas kernels for 35%

profile of v2, /device:TPU:13, one launch (start us, length us, event | category | flops | bytes accessed | tf_op | source)
XLA Modules:
  0.0 90.5 jit_solution(15021247976016641334)
XLA Ops:
  0.6 1.7 %collective-permute-start.1 = (bf16[256,1024]{1,0:T(8,128)(2,1)}, bf16[256,1024]{1,0:T(8,128)(2,1)S(1)}, u32[]{:S(2)}, u32[]{:S(2)}) collective-permute-start(bf16[256,1024]{1,0:T(8,128)(2,1)} %bitcast.5), channel_id=1, source_target_pairs={{0,8},{1,98},{2,10},{3,100},{4,12},{5,102},{6,14},{7,96},{8,16},{9... | collective-permute-start | bytes 1572872 | tf_op jit(solution)/shard_map/ppermute | solution.py:42
  2.3 2.2 %collective-permute-start.2 = (bf16[256,1024]{1,0:T(8,128)(2,1)}, bf16[256,1024]{1,0:T(8,128)(2,1)S(1)}, u32[]{:S(2)}, u32[]{:S(2)}) collective-permute-start(bf16[256,1024]{1,0:T(8,128)(2,1)} %bitcast.6), channel_id=1, source_target_pairs={{0,24},{1,102},{2,26},{3,96},{4,28},{5,98},{6,30},{7,100},{8,0},{9... | collective-permute-start | bytes 1572872 | tf_op jit(solution)/shard_map/ppermute | solution.py:42
  4.5 2.0 %pack.1 = (bf16[2,272,256]{2,1,0:T(8,128)(2,1)}, bf16[2,768,256]{2,1,0:T(8,128)(2,1)S(1)}) custom-call(bf16[2,1,1024,256]{3,2,1,0:T(8,128)(2,1)} %walkers_ref.1, s32[2]{0:T(128)} %bitcast.9, s32[2]{0:T(128)} %bitcast.10), custom_call_target="tpu_custom_call" | custom-call | tf_op jit(solution)/shard_map/pack/pallas_call | solution.py:110
  8.2 3.0 %collective-permute-done.1.a_ref = bf16[256,1024]{1,0:T(8,128)(2,1)S(1)} collective-permute-done((bf16[256,1024]{1,0:T(8,128)(2,1)}, bf16[256,1024]{1,0:T(8,128)(2,1)S(1)}, u32[]{:S(2)}, u32[]{:S(2)}) %collective-permute-start.1) | collective-permute-done | bytes 524320 | tf_op jit(solution)/shard_map/ppermute | solution.py:42
  11.3 1.5 %collective-permute-start.11 = (bf16[2,256,1024]{2,1,0:T(8,128)(2,1)S(1)}, bf16[2,256,1024]{2,1,0:T(8,128)(2,1)}, u32[]{:S(2)}, u32[]{:S(2)}) collective-permute-start(bf16[2,256,1024]{2,1,0:T(8,128)(2,1)S(1)} %stack.1.refs_1_), channel_id=1, source_target_pairs={{0,2},{1,3},{2,4},{3,5},{4,6},{5,7},{6,0},{7,1},{8,10},{9,11},{10,... | collective-permute-start | bytes 3145736 | tf_op jit(solution)/shard_map/ppermute | solution.py:42
  13.9 8.1 %collective-permute-start.6 = (bf16[2,768,256]{2,1,0:T(8,128)(2,1)S(1)}, bf16[2,768,256]{2,1,0:T(8,128)(2,1)S(1)}, u32[]{:S(2)}, u32[]{:S(2)}) collective-permute-start(bf16[2,768,256]{2,1,0:T(8,128)(2,1)S(1)} %get-tuple-element.17.own_ref), channel_id=1, source_target_pairs={{0,32},{1,33},{2,34},{3,35},{4,36},{5,37},{6,38},{7,39},{8,40},{9,... | collective-permute-start | bytes 2359304 | tf_op jit(solution)/shard_map/ppermute | solution.py:42
  22.8 6.7 %collective-permute-start.8 = (bf16[2,768,256]{2,1,0:T(8,128)(2,1)S(1)}, bf16[2,768,256]{2,1,0:T(8,128)(2,1)}, u32[]{:S(2)}, u32[]{:S(2)}) collective-permute-start(bf16[2,768,256]{2,1,0:T(8,128)(2,1)S(1)} %collective-permute-done.7.pair_ref), channel_id=1, source_target_pairs={{0,32},{1,33},{2,34},{3,35},{4,36},{5,37},{6,38},{7,39},{8,40},{9,... | collective-permute-start | bytes 2359304 | tf_op jit(solution)/shard_map/ppermute | solution.py:42
  31.3 3.6 %collective-permute-start.5 = (bf16[2,272,256]{2,1,0:T(8,128)(2,1)}, bf16[2,272,256]{2,1,0:T(8,128)(2,1)S(1)}, u32[]{:S(2)}, u32[]{:S(2)}) collective-permute-start(bf16[2,272,256]{2,1,0:T(8,128)(2,1)} %collective-permute-done.4.pair_ref), channel_id=1, source_target_pairs={{0,32},{1,33},{2,34},{3,35},{4,36},{5,37},{6,38},{7,39},{8,40},{9,... | collective-permute-start | bytes 835592 | tf_op jit(solution)/shard_map/ppermute | solution.py:42
  34.9 1.4 %collective-permute-done.5.diag_ref = bf16[2,272,256]{2,1,0:T(8,128)(2,1)S(1)} collective-permute-done((bf16[2,272,256]{2,1,0:T(8,128)(2,1)}, bf16[2,272,256]{2,1,0:T(8,128)(2,1)S(1)}, u32[]{:S(2)}, u32[]{:S(2)}) %collective-permute-start.5) | collective-permute-done | bytes 278560 | tf_op jit(solution)/shard_map/ppermute | solution.py:42
  38.2 2.7 %collective-permute-done.13.refs_0_ = bf16[256,1024]{1,0:T(8,128)(2,1)S(1)} collective-permute-done((bf16[256,1024]{1,0:T(8,128)(2,1)S(1)}, bf16[256,1024]{1,0:T(8,128)(2,1)S(1)}, u32[]{:S(2)}, u32[]{:S(2)}) %collective-permute-start.13) | collective-permute-done | bytes 524320 | tf_op jit(solution)/shard_map/ppermute | solution.py:42
  42.4 5.3 %newton.1 = (s32[4]{0:T(128)S(1)}, bf16[2,1024,256]{2,1,0:T(8,128)(2,1)S(1)}, bf16[2,256,256]{2,1,0:T(8,128)(2,1)S(1)}, f32[4,256,256]{2,1,0:T(8,128)S(1)}, f32[4,256,256]{2,1,0:T(8,128)S(1)}) custom-call(s32[1]{0:T(128)} %bitcast.2.my_ref, bf16[2,272,256]{2,1,0:T(8,128)(2,1)} %get-tuple-element.15.own_ref, ...), custom_call_target="tpu_custom_call" | custom-call | tf_op jit(solution)/shard_map/newton/pallas_call | solution.py:249
  47.7 3.4 %inverse.1 = (bf16[4,256,256]{2,1,0:T(8,128)(2,1)S(1)}, bf16[4,1024,256]{2,1,0:T(8,128)(2,1)S(1)}) custom-call(f32[4,256,256]{2,1,0:T(8,128)S(1)} %get-tuple-element.18.x_in_ref, f32[4,256,256]{2,1,0:T(8,128)S(1)} %get-tuple-element.19.r_in_ref, bf16[2,1024,256]{2,1,0:T(8,128)(2,1)S(1)} %get-tuple-element.20.new_ref.rest_1_, ...), custom_call_target="tpu_custom_call" | custom-call | tf_op jit(solution)/shard_map/inverse/pallas_call | solution.py:285
  51.8 2.1 %shard_map.59 = (bf16[4,1024,256]{2,1,0:T(8,128)(2,1)S(1)}, bf16[2,1024,256]{2,1,0:T(8,128)(2,1)S(1)}) custom-call(s32[4]{0:T(128)S(1)} %get-tuple-element.16.src_ref, bf16[2,768,256]{2,1,0:T(8,128)(2,1)S(1)} %get-tuple-element.17.own_ref, bf16[2,768,256]{2,1,0:T(8,128)(2,1)S(1)} %collective-permute-done.6.core_ref, ...), custom_call_target="tpu_custom_call", output_to_operand_aliasing={{0}: (6, {}), {1}: (7, {})} | custom-call | tf_op jit(solution)/shard_map/pallas_call | solution.py:319
  53.9 3.4 %shard_map.60 = (f32[1024,1024]{1,0:T(8,128)S(1)}, bf16[2,1,1024,256]{3,2,1,0:T(8,128)(2,1)}) custom-call(bf16[256,1024]{1,0:T(8,128)(2,1)S(1)} %own.1.refs_0_, bf16[2,256,1024]{2,1,0:T(8,128)(2,1)S(1)} %stack.1.refs_1_, bf16[4,1024,256]{2,1,0:T(8,128)(2,1)S(1)} %get-tuple-element.24.refs_2_.refs_3_, bf16[2,1024,256]{2,1,0:T(8,128)(2,1)S(1)} %get-tuple-element.25.refs_3_), custom_call_target="tpu_custom_call" | custom-call | flops 3221225472 | bytes 1572864 | tf_op jit(solution)/shard_map/pallas_call | solution.py:361
  57.3 2.7 %collective-permute-done.9.refs_2_ = bf16[256,1024]{1,0:T(8,128)(2,1)S(1)} collective-permute-done((bf16[256,1024]{1,0:T(8,128)(2,1)S(1)}, bf16[256,1024]{1,0:T(8,128)(2,1)S(1)}, u32[]{:S(2)}, u32[]{:S(2)}) %collective-permute-start.9) | collective-permute-done | bytes 524320 | tf_op jit(solution)/shard_map/ppermute | solution.py:42
  60.0 1.4 %collective-permute-start.10 = (bf16[256,1024]{1,0:T(8,128)(2,1)S(1)}, bf16[256,1024]{1,0:T(8,128)(2,1)S(1)}, u32[]{:S(2)}, u32[]{:S(2)}) collective-permute-start(bf16[256,1024]{1,0:T(8,128)(2,1)S(1)} %collective-permute-done.9.refs_2_), channel_id=1, source_target_pairs={{0,6},{1,7},{2,0},{3,1},{4,2},{5,3},{6,4},{7,5},{8,14},{9,15},{10,... | collective-permute-start | bytes 1572872 | tf_op jit(solution)/shard_map/ppermute | solution.py:42
  61.5 4.1 %collective-permute-done.14.refs_1_ = bf16[256,1024]{1,0:T(8,128)(2,1)S(1)} collective-permute-done((bf16[256,1024]{1,0:T(8,128)(2,1)S(1)}, bf16[256,1024]{1,0:T(8,128)(2,1)S(1)}, u32[]{:S(2)}, u32[]{:S(2)}) %collective-permute-start.14) | collective-permute-done | bytes 524320 | tf_op jit(solution)/shard_map/ppermute | solution.py:42
  65.9 3.4 %shard_map.61.refs_3_ = f32[1024,1024]{1,0:T(8,128)S(1)} custom-call(bf16[256,1024]{1,0:T(8,128)(2,1)S(1)} %collective-permute-done.13.refs_0_, bf16[256,1024]{1,0:T(8,128)(2,1)S(1)} %collective-permute-done.18.refs_1_, bf16[256,1024]{1,0:T(8,128)(2,1)S(1)} %collective-permute-done.9.refs_2_, ...), custom_call_target="tpu_custom_call", output_to_operand_aliasing={{}: (4, {})} | custom-call | flops 3221225472 | bytes 1572864 | tf_op jit(solution)/shard_map/pallas_call | solution.py:383
  69.4 5.8 %shard_map.62.refs_3_ = f32[1024,1024]{1,0:T(8,128)S(1)} custom-call(bf16[2,256,1024]{2,1,0:T(8,128)(2,1)} %collective-permute-done.11.refs_0_, bf16[2,256,1024]{2,1,0:T(8,128)(2,1)S(1)} %collective-permute-done.17.refs_1_, bf16[4,1024,256]{2,1,0:T(8,128)(2,1)S(1)} %get-tuple-element.24.refs_2_.refs_3_, ...), custom_call_target="tpu_custom_call", output_to_operand_aliasing={{}: (3, {})} | custom-call | flops 4294967296 | bytes 2097152 | tf_op jit(solution)/shard_map/pallas_call | solution.py:383
  75.1 2.5 %shard_map.63.refs_4_ = f32[1024,1024]{1,0:T(8,128)S(1)} custom-call(bf16[256,1024]{1,0:T(8,128)(2,1)S(1)} %collective-permute-done.16.refs_0_, bf16[256,1024]{1,0:T(8,128)(2,1)S(1)} %collective-permute-done.14.refs_1_, bf16[4,1024,256]{2,1,0:T(8,128)(2,1)S(1)} %get-tuple-element.24.refs_2_.refs_3_, ...), custom_call_target="tpu_custom_call", output_to_operand_aliasing={{}: (3, {})} | custom-call | flops 2147483648 | bytes 1048576 | tf_op jit(solution)/shard_map/pallas_call | solution.py:383
  77.6 2.3 %shard_map.65 = bf16[512,1024]{1,0:T(8,128)(2,1)S(1)} custom-call(bf16[256,1024]{1,0:T(8,128)(2,1)S(1)} %collective-permute-done.10.refs_0_, bf16[2,256,1024]{2,1,0:T(8,128)(2,1)S(1)} %collective-permute-done.12.refs_1_, bf16[256,1024]{1,0:T(8,128)(2,1)S(1)} %collective-permute-done.15.refs_2_, bf16[4,1024,256]{2,1,0:T(8,128)(2,1)S(1)} %get-tuple-element.24.refs_2_.refs_3_, ...), custom_call_target="tpu_custom_call" | custom-call | flops 2147483648 | bytes 2097152 | tf_op jit(solution)/shard_map/pallas_call | solution.py:408
  80.0 6.5 %collective-permute-start.19 = (bf16[512,1024]{1,0:T(8,128)(2,1)S(1)}, bf16[512,1024]{1,0:T(8,128)(2,1)S(1)}, u32[]{:S(2)}, u32[]{:S(2)}) collective-permute-start(bf16[512,1024]{1,0:T(8,128)(2,1)S(1)} %shard_map.65), channel_id=1, source_target_pairs={{0,32},{1,33},{2,34},{3,35},{4,36},{5,37},{6,38},{7,39},{8,40},{9,... | collective-permute-start | bytes 3145736 | tf_op jit(solution)/shard_map/ppermute | solution.py:42
  86.5 2.3 %shard_map.64.own_ref = f32[512,1024]{1,0:T(8,128)S(1)} custom-call(bf16[256,1024]{1,0:T(8,128)(2,1)S(1)} %collective-permute-done.10.refs_0_, bf16[2,256,1024]{2,1,0:T(8,128)(2,1)S(1)} %collective-permute-done.12.refs_1_, bf16[256,1024]{1,0:T(8,128)(2,1)S(1)} %collective-permute-done.15.refs_2_, ...), custom_call_target="tpu_custom_call" | custom-call | flops 2147483648 | bytes 2097152 | tf_op jit(solution)/shard_map/pallas_call | solution.py:408
  88.8 1.7 %combine.1 = f32[2,1,1024,256]{3,2,1,0:T(8,128)} custom-call(f32[512,1024]{1,0:T(8,128)S(1)} %shard_map.64.own_ref, bf16[512,1024]{1,0:T(8,128)(2,1)S(1)} %collective-permute-done.19.other_ref), custom_call_target="tpu_custom_call" | custom-call | tf_op jit(solution)/shard_map/combine/pallas_call | solution.py:427
  (31 shorter events, 9.7 us)
Async XLA Ops:
  0.6 10.6 %collective-permute-start.1 = (bf16[256,1024]{1,0:T(8,128)(2,1)}, bf16[256,1024]{1,0:T(8,128)(2,1)S(1)}, u32[]{:S(2)}, u32[]{:S(2)}) collective-permute-start(bf16[256,1024]{1,0:T(8,128)(2,1)} %bitcast.5), channel_id=1, source_target_pairs={{0,8},{1,98},{2,10},{3,100},{4,12},{5,102},{6,14},{7,96},{8,16},{9... | collective-permute-start | bytes 1572872 | tf_op jit(solution)/shard_map/ppermute | solution.py:42
  2.3 8.9 %collective-permute-start.2 = (bf16[256,1024]{1,0:T(8,128)(2,1)}, bf16[256,1024]{1,0:T(8,128)(2,1)S(1)}, u32[]{:S(2)}, u32[]{:S(2)}) collective-permute-start(bf16[256,1024]{1,0:T(8,128)(2,1)} %bitcast.6), channel_id=1, source_target_pairs={{0,24},{1,102},{2,26},{3,96},{4,28},{5,98},{6,30},{7,100},{8,0},{9... | collective-permute-start | bytes 1572872 | tf_op jit(solution)/shard_map/ppermute | solution.py:42
  6.5 16.3 %collective-permute-start.7 = (bf16[2,768,256]{2,1,0:T(8,128)(2,1)S(1)}, bf16[2,768,256]{2,1,0:T(8,128)(2,1)S(1)}, u32[]{:S(2)}, u32[]{:S(2)}) collective-permute-start(bf16[2,768,256]{2,1,0:T(8,128)(2,1)S(1)} %get-tuple-element.17.own_ref), channel_id=1, source_target_pairs={{0,64},{1,65},{2,66},{3,67},{4,68},{5,69},{6,70},{7,71},{8,72},{9,... | collective-permute-start | bytes 2359304 | tf_op jit(solution)/shard_map/ppermute | solution.py:42
  7.5 14.5 %collective-permute-start = (bf16[256,1024]{1,0:T(8,128)(2,1)}, bf16[256,1024]{1,0:T(8,128)(2,1)S(1)}, u32[]{:S(2)}, u32[]{:S(2)}) collective-permute-start(bf16[256,1024]{1,0:T(8,128)(2,1)} %bitcast.7), channel_id=1, source_target_pairs={{1,96},{3,98},{5,100},{7,102},{9,104},{11,106},{13,108},{15,110},{... | collective-permute-start | bytes 1572872 | tf_op jit(solution)/shard_map/ppermute | solution.py:42
  11.3 30.2 %collective-permute-start.11 = (bf16[2,256,1024]{2,1,0:T(8,128)(2,1)S(1)}, bf16[2,256,1024]{2,1,0:T(8,128)(2,1)}, u32[]{:S(2)}, u32[]{:S(2)}) collective-permute-start(bf16[2,256,1024]{2,1,0:T(8,128)(2,1)S(1)} %stack.1.refs_1_), channel_id=1, source_target_pairs={{0,2},{1,3},{2,4},{3,5},{4,6},{5,7},{6,0},{7,1},{8,10},{9,11},{10,... | collective-permute-start | bytes 3145736 | tf_op jit(solution)/shard_map/ppermute | solution.py:42
  12.8 17.7 %collective-permute-start.4 = (bf16[2,272,256]{2,1,0:T(8,128)(2,1)}, bf16[2,272,256]{2,1,0:T(8,128)(2,1)}, u32[]{:S(2)}, u32[]{:S(2)}) collective-permute-start(bf16[2,272,256]{2,1,0:T(8,128)(2,1)} %get-tuple-element.15.own_ref), channel_id=1, source_target_pairs={{0,64},{1,65},{2,66},{3,67},{4,68},{5,69},{6,70},{7,71},{8,72},{9,... | collective-permute-start | bytes 835592 | tf_op jit(solution)/shard_map/ppermute | solution.py:42
  13.9 23.5 %collective-permute-start.6 = (bf16[2,768,256]{2,1,0:T(8,128)(2,1)S(1)}, bf16[2,768,256]{2,1,0:T(8,128)(2,1)S(1)}, u32[]{:S(2)}, u32[]{:S(2)}) collective-permute-start(bf16[2,768,256]{2,1,0:T(8,128)(2,1)S(1)} %get-tuple-element.17.own_ref), channel_id=1, source_target_pairs={{0,32},{1,33},{2,34},{3,35},{4,36},{5,37},{6,38},{7,39},{8,40},{9,... | collective-permute-start | bytes 2359304 | tf_op jit(solution)/shard_map/ppermute | solution.py:42
  22.0 0.8 copy-start
  22.0 9.2 %collective-permute-start.3 = (bf16[2,272,256]{2,1,0:T(8,128)(2,1)}, bf16[2,272,256]{2,1,0:T(8,128)(2,1)}, u32[]{:S(2)}, u32[]{:S(2)}) collective-permute-start(bf16[2,272,256]{2,1,0:T(8,128)(2,1)} %get-tuple-element.15.own_ref), channel_id=1, source_target_pairs={{0,32},{1,33},{2,34},{3,35},{4,36},{5,37},{6,38},{7,39},{8,40},{9,... | collective-permute-start | bytes 835592 | tf_op jit(solution)/shard_map/ppermute | solution.py:42
  22.8 28.2 %collective-permute-start.8 = (bf16[2,768,256]{2,1,0:T(8,128)(2,1)S(1)}, bf16[2,768,256]{2,1,0:T(8,128)(2,1)}, u32[]{:S(2)}, u32[]{:S(2)}) collective-permute-start(bf16[2,768,256]{2,1,0:T(8,128)(2,1)S(1)} %collective-permute-done.7.pair_ref), channel_id=1, source_target_pairs={{0,32},{1,33},{2,34},{3,35},{4,36},{5,37},{6,38},{7,39},{8,40},{9,... | collective-permute-start | bytes 2359304 | tf_op jit(solution)/shard_map/ppermute | solution.py:42
  30.6 10.3 %collective-permute-start.13 = (bf16[256,1024]{1,0:T(8,128)(2,1)S(1)}, bf16[256,1024]{1,0:T(8,128)(2,1)S(1)}, u32[]{:S(2)}, u32[]{:S(2)}) collective-permute-start(bf16[256,1024]{1,0:T(8,128)(2,1)S(1)} %own.1.refs_0_), channel_id=1, source_target_pairs={{0,16},{1,17},{2,18},{3,19},{4,20},{5,21},{6,22},{7,23},{8,24},{9,... | collective-permute-start | bytes 1572872 | tf_op jit(solution)/shard_map/ppermute | solution.py:42
  31.3 5.0 %collective-permute-start.5 = (bf16[2,272,256]{2,1,0:T(8,128)(2,1)}, bf16[2,272,256]{2,1,0:T(8,128)(2,1)S(1)}, u32[]{:S(2)}, u32[]{:S(2)}) collective-permute-start(bf16[2,272,256]{2,1,0:T(8,128)(2,1)} %collective-permute-done.4.pair_ref), channel_id=1, source_target_pairs={{0,32},{1,33},{2,34},{3,35},{4,36},{5,37},{6,38},{7,39},{8,40},{9,... | collective-permute-start | bytes 835592 | tf_op jit(solution)/shard_map/ppermute | solution.py:42
  36.3 33.0 %collective-permute-start.17 = (bf16[2,256,1024]{2,1,0:T(8,128)(2,1)S(1)}, bf16[2,256,1024]{2,1,0:T(8,128)(2,1)S(1)}, u32[]{:S(2)}, u32[]{:S(2)}) collective-permute-start(bf16[2,256,1024]{2,1,0:T(8,128)(2,1)S(1)} %stack.1.refs_1_), channel_id=1, source_target_pairs={{0,6},{1,7},{2,0},{3,1},{4,2},{5,3},{6,4},{7,5},{8,14},{9,15},{10,... | collective-permute-start | bytes 3145736 | tf_op jit(solution)/shard_map/ppermute | solution.py:42
  37.4 22.6 %collective-permute-start.9 = (bf16[256,1024]{1,0:T(8,128)(2,1)S(1)}, bf16[256,1024]{1,0:T(8,128)(2,1)S(1)}, u32[]{:S(2)}, u32[]{:S(2)}) collective-permute-start(bf16[256,1024]{1,0:T(8,128)(2,1)S(1)} %own.1.refs_0_), channel_id=1, source_target_pairs={{0,6},{1,7},{2,0},{3,1},{4,2},{5,3},{6,4},{7,5},{8,14},{9,15},{10,... | collective-permute-start | bytes 1572872 | tf_op jit(solution)/shard_map/ppermute | solution.py:42
  40.9 19.1 %collective-permute-start.18 = (bf16[256,1024]{1,0:T(8,128)(2,1)S(1)}, bf16[256,1024]{1,0:T(8,128)(2,1)S(1)}, u32[]{:S(2)}, u32[]{:S(2)}) collective-permute-start(bf16[256,1024]{1,0:T(8,128)(2,1)S(1)} %own.1.refs_0_), channel_id=1, source_target_pairs={{0,2},{1,3},{2,4},{3,5},{4,6},{5,7},{6,0},{7,1},{8,10},{9,11},{10,... | collective-permute-start | bytes 1572872 | tf_op jit(solution)/shard_map/ppermute | solution.py:42
  41.5 24.1 %collective-permute-start.14 = (bf16[256,1024]{1,0:T(8,128)(2,1)S(1)}, bf16[256,1024]{1,0:T(8,128)(2,1)S(1)}, u32[]{:S(2)}, u32[]{:S(2)}) collective-permute-start(bf16[256,1024]{1,0:T(8,128)(2,1)S(1)} %collective-permute-done.13.refs_0_), channel_id=1, source_target_pairs={{0,6},{1,7},{2,0},{3,1},{4,2},{5,3},{6,4},{7,5},{8,14},{9,15},{10,... | collective-permute-start | bytes 1572872 | tf_op jit(solution)/shard_map/ppermute | solution.py:42
  51.1 26.5 %collective-permute-start.12 = (bf16[2,256,1024]{2,1,0:T(8,128)(2,1)}, bf16[2,256,1024]{2,1,0:T(8,128)(2,1)S(1)}, u32[]{:S(2)}, u32[]{:S(2)}) collective-permute-start(bf16[2,256,1024]{2,1,0:T(8,128)(2,1)} %collective-permute-done.11.refs_0_), channel_id=1, source_target_pairs={{0,2},{1,3},{2,4},{3,5},{4,6},{5,7},{6,0},{7,1},{8,10},{9,11},{10,... | collective-permute-start | bytes 3145736 | tf_op jit(solution)/shard_map/ppermute | solution.py:42
  60.0 15.1 %collective-permute-start.16 = (bf16[256,1024]{1,0:T(8,128)(2,1)S(1)}, bf16[256,1024]{1,0:T(8,128)(2,1)S(1)}, u32[]{:S(2)}, u32[]{:S(2)}) collective-permute-start(bf16[256,1024]{1,0:T(8,128)(2,1)S(1)} %collective-permute-done.13.refs_0_), channel_id=1, source_target_pairs={{0,2},{1,3},{2,4},{3,5},{4,6},{5,7},{6,0},{7,1},{8,10},{9,11},{10,... | collective-permute-start | bytes 1572872 | tf_op jit(solution)/shard_map/ppermute | solution.py:42
  60.0 17.5 %collective-permute-start.10 = (bf16[256,1024]{1,0:T(8,128)(2,1)S(1)}, bf16[256,1024]{1,0:T(8,128)(2,1)S(1)}, u32[]{:S(2)}, u32[]{:S(2)}) collective-permute-start(bf16[256,1024]{1,0:T(8,128)(2,1)S(1)} %collective-permute-done.9.refs_2_), channel_id=1, source_target_pairs={{0,6},{1,7},{2,0},{3,1},{4,2},{5,3},{6,4},{7,5},{8,14},{9,15},{10,... | collective-permute-start | bytes 1572872 | tf_op jit(solution)/shard_map/ppermute | solution.py:42
  65.6 12.0 %collective-permute-start.15 = (bf16[256,1024]{1,0:T(8,128)(2,1)S(1)}, bf16[256,1024]{1,0:T(8,128)(2,1)S(1)}, u32[]{:S(2)}, u32[]{:S(2)}) collective-permute-start(bf16[256,1024]{1,0:T(8,128)(2,1)S(1)} %collective-permute-done.14.refs_1_), channel_id=1, source_target_pairs={{0,6},{1,7},{2,0},{3,1},{4,2},{5,3},{6,4},{7,5},{8,14},{9,15},{10,... | collective-permute-start | bytes 1572872 | tf_op jit(solution)/shard_map/ppermute | solution.py:42
  80.0 8.8 %collective-permute-start.19 = (bf16[512,1024]{1,0:T(8,128)(2,1)S(1)}, bf16[512,1024]{1,0:T(8,128)(2,1)S(1)}, u32[]{:S(2)}, u32[]{:S(2)}) collective-permute-start(bf16[512,1024]{1,0:T(8,128)(2,1)S(1)} %shard_map.65), channel_id=1, source_target_pairs={{0,32},{1,33},{2,34},{3,35},{4,36},{5,37},{6,38},{7,39},{8,40},{9,... | collective-permute-start | bytes 3145736 | tf_op jit(solution)/shard_map/ppermute | solution.py:42

commit v3 on v2

--- a/solution.py
+++ b/solution.py
@@ -113,7 +113,7 @@
         out_specs=[VM, VM],
         out_shape=[pltpu.VMEM((2, NEL + 16, NEL), BF16), pltpu.VMEM((2, M - NEL, NEL), BF16)],
         scratch_shapes=[pltpu.SMEM((2, 2), jnp.int32), pltpu.SemaphoreType.DMA((4,))],
-        compiler_params=pltpu.CompilerParams(vmem_limit_bytes=4 * MIB),
+        compiler_params=pltpu.CompilerParams(vmem_limit_bytes=2 * MIB),
         name="pack",
     )(held(walkers), held(counts[:, 0]), held(slots[:, 0]))
 
@@ -139,7 +139,7 @@
         out_specs=VM,
         out_shape=pltpu.VMEM(kept.shape, BF16),
         scratch_shapes=[pltpu.SemaphoreType.DMA],
-        compiler_params=pltpu.CompilerParams(vmem_limit_bytes=2 * MIB),
+        compiler_params=pltpu.CompilerParams(vmem_limit_bytes=1 * MIB),
         name="own",
     )(local, held(kept), held(swapped))
 
@@ -163,7 +163,7 @@
         out_specs=VM,
         out_shape=pltpu.VMEM((2,) + a.shape, BF16),
         scratch_shapes=[pltpu.SemaphoreType.DMA((2,))],
-        compiler_params=pltpu.CompilerParams(vmem_limit_bytes=4 * MIB),
+        compiler_params=pltpu.CompilerParams(vmem_limit_bytes=1 * MIB),
         name="stack",
     )(a, b)
 
@@ -258,7 +258,7 @@
             pltpu.VMEM((4, NEL, NEL), F32),
         ],
         scratch_shapes=[pltpu.VMEM((16, NEL, NEL), BF16)],
-        compiler_params=pltpu.CompilerParams(vmem_limit_bytes=16 * MIB),
+        compiler_params=pltpu.CompilerParams(vmem_limit_bytes=6 * MIB),
         name="newton",
     )(my, own, core, pair, diag)
 
@@ -292,7 +292,7 @@
             pltpu.VMEM((4, NEL, NEL), F32),
             pltpu.VMEM((16, NEL, NEL), BF16),
         ],
-        compiler_params=pltpu.CompilerParams(vmem_limit_bytes=16 * MIB),
+        compiler_params=pltpu.CompilerParams(vmem_limit_bytes=6 * MIB),
         name="inverse",
     )(x, r, new, c)
 
@@ -323,7 +323,7 @@
         out_shape=[pltpu.VMEM((4, M, NEL), BF16), pltpu.VMEM((2, M, NEL), BF16)],
         scratch_shapes=[pltpu.VMEM((2, rows, NEL), BF16)],
         input_output_aliases={6: 0, 7: 1},
-        compiler_params=pltpu.CompilerParams(vmem_limit_bytes=16 * MIB),
+        compiler_params=pltpu.CompilerParams(vmem_limit_bytes=4 * MIB),
     )(src, own, core, pair, diag, inv, *carried)
 
 
@@ -364,7 +364,7 @@
         out_specs=[VM, pl.BlockSpec(memory_space=pl.ANY)],
         out_shape=[pltpu.VMEM((4 * NEL, M), F32), jax.ShapeDtypeStruct((2, 1, M, NEL), BF16)],
         scratch_shapes=[pltpu.VMEM((4 * NEL, count * NEL), BF16), pltpu.SemaphoreType.DMA],
-        compiler_params=pltpu.CompilerParams(vmem_limit_bytes=24 * MIB),
+        compiler_params=pltpu.CompilerParams(vmem_limit_bytes=12 * MIB),
         cost_estimate=pl.CostEstimate(
             flops=count * 16 * NEL * NEL * M, transcendentals=0, bytes_accessed=count * MIB // 2
         ),
@@ -387,7 +387,7 @@
         out_shape=pltpu.VMEM((4 * NEL, M), F32),
         scratch_shapes=[pltpu.VMEM((4 * NEL, count * NEL), BF16)],
         input_output_aliases={n + 1: 0},
-        compiler_params=pltpu.CompilerParams(vmem_limit_bytes=24 * MIB),
+        compiler_params=pltpu.CompilerParams(vmem_limit_bytes=12 * MIB),
         cost_estimate=pl.CostEstimate(
             flops=count * 16 * NEL * NEL * M, transcendentals=0, bytes_accessed=count * MIB // 2
         ),
@@ -411,7 +411,7 @@
         out_specs=VM,
         out_shape=out_shape,
         scratch_shapes=[pltpu.VMEM((2 * NEL, count * NEL), BF16)],
-        compiler_params=pltpu.CompilerParams(vmem_limit_bytes=24 * MIB),
+        compiler_params=pltpu.CompilerParams(vmem_limit_bytes=10 * MIB),
         cost_estimate=pl.CostEstimate(
             flops=count * 8 * NEL * NEL * M, transcendentals=0, bytes_accessed=count * MIB // 2
         ),
@@ -430,7 +430,7 @@
         in_specs=[part, part],
         out_specs=pl.BlockSpec((1, 1, M, NEL), lambda w: (w, 0, 0, 0)),
         out_shape=jax.ShapeDtypeStruct((2, 1, M, NEL), F32),
-        compiler_params=pltpu.CompilerParams(vmem_limit_bytes=16 * MIB),
+        compiler_params=pltpu.CompilerParams(vmem_limit_bytes=8 * MIB),
         name="combine",
     )(own, other)
 
@@ -470,8 +470,8 @@
     running, combed = first_part([f[0, 0], sides], green, new)
     running = main_part([f[2, 0], f[0, -1], f[0, 1]], green, running)
     running = main_part([sides_below, sides_above], green, running)
-    running = main_part([f[2, -1], f[2, 1]], green, running)
-    blocks = [f[0, 2], sides_far, f[2, 2]]
+    running = main_part([f[2, -1], f[2, 1], f[0, 2]], green, running)
+    blocks = [sides_far, f[2, 2]]
     half = (2 * NEL, M)
     other = to_core(last_part(blocks, green, running, 2, jax.ShapeDtypeStruct(half, BF16)))
     own = last_part(blocks, green, running, 0, pltpu.VMEM(half, F32))

time: 90.8 us -> 91.2 us (level)
    pallas_call x2, Pallas kernels: 4.67 us -> 3.59 us  [last_part(): pl.pallas_call(functools.partial(last_kernel, n=n, low=low), in_specs=[VM...]
    pallas_call x3, Pallas kernels: 11.7 us -> 12.7 us  [main_part(): pl.pallas_call(functools.partial(main_kernel, n=n), in_specs=[VM] * (n +...]
  transfers between devices with their start and end apart: 20 -> 20, of which waited for: 5 -> 6; matrix products, arithmetic and copies ran while one was open for 0% -> 0% of each run, Pallas kernels for 35% -> 35%
where the time goes in v3:
time: 91.2 us; the launch traced here: 90.9 us
  starting transfers between devices  40.2 us (44%)
  Pallas kernels  35.2 us (39%)
  waiting for transfers between devices  14.6 us (16%)
    ppermute x20, starting transfers between devices, moved(): return lax.ppermute(x, ('walk', 'chol'), pairs)  40.2 us
    ppermute x20, waiting for transfers between devices, moved(): return lax.ppermute(x, ('walk', 'chol'), pairs)  14.6 us
    pallas_call x3, Pallas kernels, main_part(): pl.pallas_call(functools.partial(main_kernel, n=n), in_specs=[VM] * (n +...  12.7 us
    pallas_call x1, Pallas kernels, newton(): pl.pallas_call(newton_kernel, in_specs=[SM, VM, VM, VM, VM], out_specs=[S...  5.32 us
    pallas_call x2, Pallas kernels, last_part(): pl.pallas_call(functools.partial(last_kernel, n=n, low=low), in_specs=[VM...  3.59 us
    pallas_call x1, Pallas kernels, first_part(): pl.pallas_call(functools.partial(first_kernel, n=n), in_specs=[VM] * (n +...  3.43 us
    pallas_call x1, Pallas kernels, inverse(): pl.pallas_call(inverse_kernel, in_specs=[VM] * 4, out_specs=[VM, VM], out...  3.36 us
    pallas_call x1, Pallas kernels, green_piece(): pl.pallas_call(functools.partial(green_kernel, at=at, rows=rows), in_spec...  2.09 us
  transfers between devices with their start and end apart: 20, of which 6 were waited for; matrix products, arithmetic and copies ran while one was open for 0% of the time, Pallas kernels for 35%

profile of v3, /device:TPU:13, one launch (start us, length us, event | category | flops | bytes accessed | tf_op | source)
XLA Modules:
  0.0 90.9 jit_solution(2768773421431197586)
XLA Ops:
  0.6 1.7 %collective-permute-start.1 = (bf16[256,1024]{1,0:T(8,128)(2,1)}, bf16[256,1024]{1,0:T(8,128)(2,1)S(1)}, u32[]{:S(2)}, u32[]{:S(2)}) collective-permute-start(bf16[256,1024]{1,0:T(8,128)(2,1)} %bitcast.5), channel_id=1, source_target_pairs={{0,8},{1,98},{2,10},{3,100},{4,12},{5,102},{6,14},{7,96},{8,16},{9... | collective-permute-start | bytes 1572872 | tf_op jit(solution)/shard_map/ppermute | solution.py:42
  2.3 2.2 %collective-permute-start.2 = (bf16[256,1024]{1,0:T(8,128)(2,1)}, bf16[256,1024]{1,0:T(8,128)(2,1)S(1)}, u32[]{:S(2)}, u32[]{:S(2)}) collective-permute-start(bf16[256,1024]{1,0:T(8,128)(2,1)} %bitcast.6), channel_id=1, source_target_pairs={{0,24},{1,102},{2,26},{3,96},{4,28},{5,98},{6,30},{7,100},{8,0},{9... | collective-permute-start | bytes 1572872 | tf_op jit(solution)/shard_map/ppermute | solution.py:42
  4.5 2.0 %pack.1 = (bf16[2,272,256]{2,1,0:T(8,128)(2,1)}, bf16[2,768,256]{2,1,0:T(8,128)(2,1)S(1)}) custom-call(bf16[2,1,1024,256]{3,2,1,0:T(8,128)(2,1)} %walkers_ref.1, s32[2]{0:T(128)} %bitcast.9, s32[2]{0:T(128)} %bitcast.10), custom_call_target="tpu_custom_call" | custom-call | tf_op jit(solution)/shard_map/pack/pallas_call | solution.py:110
  8.2 3.0 %collective-permute-done.1.a_ref = bf16[256,1024]{1,0:T(8,128)(2,1)S(1)} collective-permute-done((bf16[256,1024]{1,0:T(8,128)(2,1)}, bf16[256,1024]{1,0:T(8,128)(2,1)S(1)}, u32[]{:S(2)}, u32[]{:S(2)}) %collective-permute-start.1) | collective-permute-done | bytes 524320 | tf_op jit(solution)/shard_map/ppermute | solution.py:42
  11.3 1.5 %collective-permute-start.9 = (bf16[2,256,1024]{2,1,0:T(8,128)(2,1)S(1)}, bf16[2,256,1024]{2,1,0:T(8,128)(2,1)}, u32[]{:S(2)}, u32[]{:S(2)}) collective-permute-start(bf16[2,256,1024]{2,1,0:T(8,128)(2,1)S(1)} %stack.1.refs_1_), channel_id=1, source_target_pairs={{0,2},{1,3},{2,4},{3,5},{4,6},{5,7},{6,0},{7,1},{8,10},{9,11},{10,... | collective-permute-start | bytes 3145736 | tf_op jit(solution)/shard_map/ppermute | solution.py:42
  13.9 8.1 %collective-permute-start.6 = (bf16[2,768,256]{2,1,0:T(8,128)(2,1)S(1)}, bf16[2,768,256]{2,1,0:T(8,128)(2,1)S(1)}, u32[]{:S(2)}, u32[]{:S(2)}) collective-permute-start(bf16[2,768,256]{2,1,0:T(8,128)(2,1)S(1)} %get-tuple-element.17.own_ref), channel_id=1, source_target_pairs={{0,32},{1,33},{2,34},{3,35},{4,36},{5,37},{6,38},{7,39},{8,40},{9,... | collective-permute-start | bytes 2359304 | tf_op jit(solution)/shard_map/ppermute | solution.py:42
  22.8 6.7 %collective-permute-start.8 = (bf16[2,768,256]{2,1,0:T(8,128)(2,1)S(1)}, bf16[2,768,256]{2,1,0:T(8,128)(2,1)}, u32[]{:S(2)}, u32[]{:S(2)}) collective-permute-start(bf16[2,768,256]{2,1,0:T(8,128)(2,1)S(1)} %collective-permute-done.7.pair_ref), channel_id=1, source_target_pairs={{0,32},{1,33},{2,34},{3,35},{4,36},{5,37},{6,38},{7,39},{8,40},{9,... | collective-permute-start | bytes 2359304 | tf_op jit(solution)/shard_map/ppermute | solution.py:42
  31.3 3.6 %collective-permute-start.5 = (bf16[2,272,256]{2,1,0:T(8,128)(2,1)}, bf16[2,272,256]{2,1,0:T(8,128)(2,1)S(1)}, u32[]{:S(2)}, u32[]{:S(2)}) collective-permute-start(bf16[2,272,256]{2,1,0:T(8,128)(2,1)} %collective-permute-done.4.pair_ref), channel_id=1, source_target_pairs={{0,32},{1,33},{2,34},{3,35},{4,36},{5,37},{6,38},{7,39},{8,40},{9,... | collective-permute-start | bytes 835592 | tf_op jit(solution)/shard_map/ppermute | solution.py:42
  34.9 1.4 %collective-permute-done.5.diag_ref = bf16[2,272,256]{2,1,0:T(8,128)(2,1)S(1)} collective-permute-done((bf16[2,272,256]{2,1,0:T(8,128)(2,1)}, bf16[2,272,256]{2,1,0:T(8,128)(2,1)S(1)}, u32[]{:S(2)}, u32[]{:S(2)}) %collective-permute-start.5) | collective-permute-done | bytes 278560 | tf_op jit(solution)/shard_map/ppermute | solution.py:42
  38.2 2.7 %collective-permute-done.11.refs_0_ = bf16[256,1024]{1,0:T(8,128)(2,1)S(1)} collective-permute-done((bf16[256,1024]{1,0:T(8,128)(2,1)S(1)}, bf16[256,1024]{1,0:T(8,128)(2,1)S(1)}, u32[]{:S(2)}, u32[]{:S(2)}) %collective-permute-start.11) | collective-permute-done | bytes 524320 | tf_op jit(solution)/shard_map/ppermute | solution.py:42
  42.4 5.3 %newton.1 = (s32[4]{0:T(128)S(1)}, bf16[2,1024,256]{2,1,0:T(8,128)(2,1)S(1)}, bf16[2,256,256]{2,1,0:T(8,128)(2,1)S(1)}, f32[4,256,256]{2,1,0:T(8,128)S(1)}, f32[4,256,256]{2,1,0:T(8,128)S(1)}) custom-call(s32[1]{0:T(128)} %bitcast.2.my_ref, bf16[2,272,256]{2,1,0:T(8,128)(2,1)} %get-tuple-element.15.own_ref, ...), custom_call_target="tpu_custom_call" | custom-call | tf_op jit(solution)/shard_map/newton/pallas_call | solution.py:249
  47.7 3.4 %inverse.1 = (bf16[4,256,256]{2,1,0:T(8,128)(2,1)S(1)}, bf16[4,1024,256]{2,1,0:T(8,128)(2,1)S(1)}) custom-call(f32[4,256,256]{2,1,0:T(8,128)S(1)} %get-tuple-element.18.x_in_ref, f32[4,256,256]{2,1,0:T(8,128)S(1)} %get-tuple-element.19.r_in_ref, bf16[2,1024,256]{2,1,0:T(8,128)(2,1)S(1)} %get-tuple-element.20.new_ref.rest_1_, ...), custom_call_target="tpu_custom_call" | custom-call | tf_op jit(solution)/shard_map/inverse/pallas_call | solution.py:285
  51.8 2.1 %shard_map.59 = (bf16[4,1024,256]{2,1,0:T(8,128)(2,1)S(1)}, bf16[2,1024,256]{2,1,0:T(8,128)(2,1)S(1)}) custom-call(s32[4]{0:T(128)S(1)} %get-tuple-element.16.src_ref, bf16[2,768,256]{2,1,0:T(8,128)(2,1)S(1)} %get-tuple-element.17.own_ref, bf16[2,768,256]{2,1,0:T(8,128)(2,1)S(1)} %collective-permute-done.6.core_ref, ...), custom_call_target="tpu_custom_call", output_to_operand_aliasing={{0}: (6, {}), {1}: (7, {})} | custom-call | tf_op jit(solution)/shard_map/pallas_call | solution.py:319
  53.9 3.4 %shard_map.60 = (f32[1024,1024]{1,0:T(8,128)S(1)}, bf16[2,1,1024,256]{3,2,1,0:T(8,128)(2,1)}) custom-call(bf16[256,1024]{1,0:T(8,128)(2,1)S(1)} %own.1.refs_0_, bf16[2,256,1024]{2,1,0:T(8,128)(2,1)S(1)} %stack.1.refs_1_, bf16[4,1024,256]{2,1,0:T(8,128)(2,1)S(1)} %get-tuple-element.24.refs_2_.refs_3_, bf16[2,1024,256]{2,1,0:T(8,128)(2,1)S(1)} %get-tuple-element.25.refs_3_), custom_call_target="tpu_custom_call" | custom-call | flops 3221225472 | bytes 1572864 | tf_op jit(solution)/shard_map/pallas_call | solution.py:361
  57.3 2.7 %collective-permute-done.15.refs_2_ = bf16[256,1024]{1,0:T(8,128)(2,1)S(1)} collective-permute-done((bf16[256,1024]{1,0:T(8,128)(2,1)S(1)}, bf16[256,1024]{1,0:T(8,128)(2,1)S(1)}, u32[]{:S(2)}, u32[]{:S(2)}) %collective-permute-start.15) | collective-permute-done | bytes 524320 | tf_op jit(solution)/shard_map/ppermute | solution.py:42
  60.0 1.4 %collective-permute-start.16 = (bf16[256,1024]{1,0:T(8,128)(2,1)S(1)}, bf16[256,1024]{1,0:T(8,128)(2,1)S(1)}, u32[]{:S(2)}, u32[]{:S(2)}) collective-permute-start(bf16[256,1024]{1,0:T(8,128)(2,1)S(1)} %collective-permute-done.15.refs_2_), channel_id=1, source_target_pairs={{0,6},{1,7},{2,0},{3,1},{4,2},{5,3},{6,4},{7,5},{8,14},{9,15},{10,... | collective-permute-start | bytes 1572872 | tf_op jit(solution)/shard_map/ppermute | solution.py:42
  61.5 4.1 %collective-permute-done.12.refs_1_ = bf16[256,1024]{1,0:T(8,128)(2,1)S(1)} collective-permute-done((bf16[256,1024]{1,0:T(8,128)(2,1)S(1)}, bf16[256,1024]{1,0:T(8,128)(2,1)S(1)}, u32[]{:S(2)}, u32[]{:S(2)}) %collective-permute-start.12) | collective-permute-done | bytes 524320 | tf_op jit(solution)/shard_map/ppermute | solution.py:42
  65.9 3.4 %shard_map.61.refs_3_ = f32[1024,1024]{1,0:T(8,128)S(1)} custom-call(bf16[256,1024]{1,0:T(8,128)(2,1)S(1)} %collective-permute-done.11.refs_0_, bf16[256,1024]{1,0:T(8,128)(2,1)S(1)} %collective-permute-done.18.refs_1_, bf16[256,1024]{1,0:T(8,128)(2,1)S(1)} %collective-permute-done.15.refs_2_, ...), custom_call_target="tpu_custom_call", output_to_operand_aliasing={{}: (4, {})} | custom-call | flops 3221225472 | bytes 1572864 | tf_op jit(solution)/shard_map/pallas_call | solution.py:383
  69.4 5.8 %shard_map.62.refs_4_ = f32[1024,1024]{1,0:T(8,128)S(1)} custom-call(bf16[2,256,1024]{2,1,0:T(8,128)(2,1)} %collective-permute-done.9.refs_0_, bf16[2,256,1024]{2,1,0:T(8,128)(2,1)S(1)} %collective-permute-done.17.refs_1_, bf16[4,1024,256]{2,1,0:T(8,128)(2,1)S(1)} %get-tuple-element.24.refs_2_.refs_3_, ...), custom_call_target="tpu_custom_call", output_to_operand_aliasing={{}: (3, {})} | custom-call | flops 4294967296 | bytes 2097152 | tf_op jit(solution)/shard_map/pallas_call | solution.py:383
  75.1 3.5 %shard_map.63.refs_3_ = f32[1024,1024]{1,0:T(8,128)S(1)} custom-call(bf16[256,1024]{1,0:T(8,128)(2,1)S(1)} %collective-permute-done.14.refs_0_, bf16[256,1024]{1,0:T(8,128)(2,1)S(1)} %collective-permute-done.12.refs_1_, bf16[256,1024]{1,0:T(8,128)(2,1)S(1)} %collective-permute-done.16.refs_2_, ...), custom_call_target="tpu_custom_call", output_to_operand_aliasing={{}: (4, {})} | custom-call | flops 3221225472 | bytes 1572864 | tf_op jit(solution)/shard_map/pallas_call | solution.py:383
  78.6 1.8 %shard_map.65 = bf16[512,1024]{1,0:T(8,128)(2,1)S(1)} custom-call(bf16[2,256,1024]{2,1,0:T(8,128)(2,1)S(1)} %collective-permute-done.10.refs_0_, bf16[256,1024]{1,0:T(8,128)(2,1)S(1)} %collective-permute-done.13.refs_1_, bf16[4,1024,256]{2,1,0:T(8,128)(2,1)S(1)} %get-tuple-element.24.refs_2_.refs_3_, f32[1024,1024]{1,0:T(8,128)S(1)} %shard_map.63.refs_3_), custom_call_target="tpu_custom_call" | custom-call | flops 1610612736 | bytes 1572864 | tf_op jit(solution)/shard_map/pallas_call | solution.py:408
  80.4 6.5 %collective-permute-start.19 = (bf16[512,1024]{1,0:T(8,128)(2,1)S(1)}, bf16[512,1024]{1,0:T(8,128)(2,1)S(1)}, u32[]{:S(2)}, u32[]{:S(2)}) collective-permute-start(bf16[512,1024]{1,0:T(8,128)(2,1)S(1)} %shard_map.65), channel_id=1, source_target_pairs={{0,32},{1,33},{2,34},{3,35},{4,36},{5,37},{6,38},{7,39},{8,40},{9,... | collective-permute-start | bytes 3145736 | tf_op jit(solution)/shard_map/ppermute | solution.py:42
  86.9 1.8 %shard_map.64.own_ref = f32[512,1024]{1,0:T(8,128)S(1)} custom-call(bf16[2,256,1024]{2,1,0:T(8,128)(2,1)S(1)} %collective-permute-done.10.refs_0_, bf16[256,1024]{1,0:T(8,128)(2,1)S(1)} %collective-permute-done.13.refs_1_, bf16[4,1024,256]{2,1,0:T(8,128)(2,1)S(1)} %get-tuple-element.24.refs_2_.refs_3_, f32[1024,1024]{1,0:T(8,128)S(1)} %shard_map.63.refs_3_), custom_call_target="tpu_custom_call" | custom-call | flops 1610612736 | bytes 1572864 | tf_op jit(solution)/shard_map/pallas_call | solution.py:408
  89.2 1.7 %combine.1 = f32[2,1,1024,256]{3,2,1,0:T(8,128)} custom-call(f32[512,1024]{1,0:T(8,128)S(1)} %shard_map.64.own_ref, bf16[512,1024]{1,0:T(8,128)(2,1)S(1)} %collective-permute-done.19.other_ref), custom_call_target="tpu_custom_call" | custom-call | tf_op jit(solution)/shard_map/combine/pallas_call | solution.py:427
  (31 shorter events, 10.2 us)
Async XLA Ops:
  0.6 10.6 %collective-permute-start.1 = (bf16[256,1024]{1,0:T(8,128)(2,1)}, bf16[256,1024]{1,0:T(8,128)(2,1)S(1)}, u32[]{:S(2)}, u32[]{:S(2)}) collective-permute-start(bf16[256,1024]{1,0:T(8,128)(2,1)} %bitcast.5), channel_id=1, source_target_pairs={{0,8},{1,98},{2,10},{3,100},{4,12},{5,102},{6,14},{7,96},{8,16},{9... | collective-permute-start | bytes 1572872 | tf_op jit(solution)/shard_map/ppermute | solution.py:42
  2.3 8.9 %collective-permute-start.2 = (bf16[256,1024]{1,0:T(8,128)(2,1)}, bf16[256,1024]{1,0:T(8,128)(2,1)S(1)}, u32[]{:S(2)}, u32[]{:S(2)}) collective-permute-start(bf16[256,1024]{1,0:T(8,128)(2,1)} %bitcast.6), channel_id=1, source_target_pairs={{0,24},{1,102},{2,26},{3,96},{4,28},{5,98},{6,30},{7,100},{8,0},{9... | collective-permute-start | bytes 1572872 | tf_op jit(solution)/shard_map/ppermute | solution.py:42
  6.5 16.3 %collective-permute-start.7 = (bf16[2,768,256]{2,1,0:T(8,128)(2,1)S(1)}, bf16[2,768,256]{2,1,0:T(8,128)(2,1)S(1)}, u32[]{:S(2)}, u32[]{:S(2)}) collective-permute-start(bf16[2,768,256]{2,1,0:T(8,128)(2,1)S(1)} %get-tuple-element.17.own_ref), channel_id=1, source_target_pairs={{0,64},{1,65},{2,66},{3,67},{4,68},{5,69},{6,70},{7,71},{8,72},{9,... | collective-permute-start | bytes 2359304 | tf_op jit(solution)/shard_map/ppermute | solution.py:42
  7.5 14.5 %collective-permute-start = (bf16[256,1024]{1,0:T(8,128)(2,1)}, bf16[256,1024]{1,0:T(8,128)(2,1)S(1)}, u32[]{:S(2)}, u32[]{:S(2)}) collective-permute-start(bf16[256,1024]{1,0:T(8,128)(2,1)} %bitcast.7), channel_id=1, source_target_pairs={{1,96},{3,98},{5,100},{7,102},{9,104},{11,106},{13,108},{15,110},{... | collective-permute-start | bytes 1572872 | tf_op jit(solution)/shard_map/ppermute | solution.py:42
  11.3 30.2 %collective-permute-start.9 = (bf16[2,256,1024]{2,1,0:T(8,128)(2,1)S(1)}, bf16[2,256,1024]{2,1,0:T(8,128)(2,1)}, u32[]{:S(2)}, u32[]{:S(2)}) collective-permute-start(bf16[2,256,1024]{2,1,0:T(8,128)(2,1)S(1)} %stack.1.refs_1_), channel_id=1, source_target_pairs={{0,2},{1,3},{2,4},{3,5},{4,6},{5,7},{6,0},{7,1},{8,10},{9,11},{10,... | collective-permute-start | bytes 3145736 | tf_op jit(solution)/shard_map/ppermute | solution.py:42
  12.8 17.7 %collective-permute-start.4 = (bf16[2,272,256]{2,1,0:T(8,128)(2,1)}, bf16[2,272,256]{2,1,0:T(8,128)(2,1)}, u32[]{:S(2)}, u32[]{:S(2)}) collective-permute-start(bf16[2,272,256]{2,1,0:T(8,128)(2,1)} %get-tuple-element.15.own_ref), channel_id=1, source_target_pairs={{0,64},{1,65},{2,66},{3,67},{4,68},{5,69},{6,70},{7,71},{8,72},{9,... | collective-permute-start | bytes 835592 | tf_op jit(solution)/shard_map/ppermute | solution.py:42
  13.9 23.5 %collective-permute-start.6 = (bf16[2,768,256]{2,1,0:T(8,128)(2,1)S(1)}, bf16[2,768,256]{2,1,0:T(8,128)(2,1)S(1)}, u32[]{:S(2)}, u32[]{:S(2)}) collective-permute-start(bf16[2,768,256]{2,1,0:T(8,128)(2,1)S(1)} %get-tuple-element.17.own_ref), channel_id=1, source_target_pairs={{0,32},{1,33},{2,34},{3,35},{4,36},{5,37},{6,38},{7,39},{8,40},{9,... | collective-permute-start | bytes 2359304 | tf_op jit(solution)/shard_map/ppermute | solution.py:42
  22.0 0.8 copy-start
  22.0 9.2 %collective-permute-start.3 = (bf16[2,272,256]{2,1,0:T(8,128)(2,1)}, bf16[2,272,256]{2,1,0:T(8,128)(2,1)}, u32[]{:S(2)}, u32[]{:S(2)}) collective-permute-start(bf16[2,272,256]{2,1,0:T(8,128)(2,1)} %get-tuple-element.15.own_ref), channel_id=1, source_target_pairs={{0,32},{1,33},{2,34},{3,35},{4,36},{5,37},{6,38},{7,39},{8,40},{9,... | collective-permute-start | bytes 835592 | tf_op jit(solution)/shard_map/ppermute | solution.py:42
  22.8 28.2 %collective-permute-start.8 = (bf16[2,768,256]{2,1,0:T(8,128)(2,1)S(1)}, bf16[2,768,256]{2,1,0:T(8,128)(2,1)}, u32[]{:S(2)}, u32[]{:S(2)}) collective-permute-start(bf16[2,768,256]{2,1,0:T(8,128)(2,1)S(1)} %collective-permute-done.7.pair_ref), channel_id=1, source_target_pairs={{0,32},{1,33},{2,34},{3,35},{4,36},{5,37},{6,38},{7,39},{8,40},{9,... | collective-permute-start | bytes 2359304 | tf_op jit(solution)/shard_map/ppermute | solution.py:42
  30.6 10.3 %collective-permute-start.11 = (bf16[256,1024]{1,0:T(8,128)(2,1)S(1)}, bf16[256,1024]{1,0:T(8,128)(2,1)S(1)}, u32[]{:S(2)}, u32[]{:S(2)}) collective-permute-start(bf16[256,1024]{1,0:T(8,128)(2,1)S(1)} %own.1.refs_0_), channel_id=1, source_target_pairs={{0,16},{1,17},{2,18},{3,19},{4,20},{5,21},{6,22},{7,23},{8,24},{9,... | collective-permute-start | bytes 1572872 | tf_op jit(solution)/shard_map/ppermute | solution.py:42
  31.3 5.0 %collective-permute-start.5 = (bf16[2,272,256]{2,1,0:T(8,128)(2,1)}, bf16[2,272,256]{2,1,0:T(8,128)(2,1)S(1)}, u32[]{:S(2)}, u32[]{:S(2)}) collective-permute-start(bf16[2,272,256]{2,1,0:T(8,128)(2,1)} %collective-permute-done.4.pair_ref), channel_id=1, source_target_pairs={{0,32},{1,33},{2,34},{3,35},{4,36},{5,37},{6,38},{7,39},{8,40},{9,... | collective-permute-start | bytes 835592 | tf_op jit(solution)/shard_map/ppermute | solution.py:42
  36.3 33.0 %collective-permute-start.17 = (bf16[2,256,1024]{2,1,0:T(8,128)(2,1)S(1)}, bf16[2,256,1024]{2,1,0:T(8,128)(2,1)S(1)}, u32[]{:S(2)}, u32[]{:S(2)}) collective-permute-start(bf16[2,256,1024]{2,1,0:T(8,128)(2,1)S(1)} %stack.1.refs_1_), channel_id=1, source_target_pairs={{0,6},{1,7},{2,0},{3,1},{4,2},{5,3},{6,4},{7,5},{8,14},{9,15},{10,... | collective-permute-start | bytes 3145736 | tf_op jit(solution)/shard_map/ppermute | solution.py:42
  37.4 22.6 %collective-permute-start.15 = (bf16[256,1024]{1,0:T(8,128)(2,1)S(1)}, bf16[256,1024]{1,0:T(8,128)(2,1)S(1)}, u32[]{:S(2)}, u32[]{:S(2)}) collective-permute-start(bf16[256,1024]{1,0:T(8,128)(2,1)S(1)} %own.1.refs_0_), channel_id=1, source_target_pairs={{0,6},{1,7},{2,0},{3,1},{4,2},{5,3},{6,4},{7,5},{8,14},{9,15},{10,... | collective-permute-start | bytes 1572872 | tf_op jit(solution)/shard_map/ppermute | solution.py:42
  40.9 19.1 %collective-permute-start.18 = (bf16[256,1024]{1,0:T(8,128)(2,1)S(1)}, bf16[256,1024]{1,0:T(8,128)(2,1)S(1)}, u32[]{:S(2)}, u32[]{:S(2)}) collective-permute-start(bf16[256,1024]{1,0:T(8,128)(2,1)S(1)} %own.1.refs_0_), channel_id=1, source_target_pairs={{0,2},{1,3},{2,4},{3,5},{4,6},{5,7},{6,0},{7,1},{8,10},{9,11},{10,... | collective-permute-start | bytes 1572872 | tf_op jit(solution)/shard_map/ppermute | solution.py:42
  41.5 24.1 %collective-permute-start.12 = (bf16[256,1024]{1,0:T(8,128)(2,1)S(1)}, bf16[256,1024]{1,0:T(8,128)(2,1)S(1)}, u32[]{:S(2)}, u32[]{:S(2)}) collective-permute-start(bf16[256,1024]{1,0:T(8,128)(2,1)S(1)} %collective-permute-done.11.refs_0_), channel_id=1, source_target_pairs={{0,6},{1,7},{2,0},{3,1},{4,2},{5,3},{6,4},{7,5},{8,14},{9,15},{10,... | collective-permute-start | bytes 1572872 | tf_op jit(solution)/shard_map/ppermute | solution.py:42
  51.1 27.5 %collective-permute-start.10 = (bf16[2,256,1024]{2,1,0:T(8,128)(2,1)}, bf16[2,256,1024]{2,1,0:T(8,128)(2,1)S(1)}, u32[]{:S(2)}, u32[]{:S(2)}) collective-permute-start(bf16[2,256,1024]{2,1,0:T(8,128)(2,1)} %collective-permute-done.9.refs_0_), channel_id=1, source_target_pairs={{0,2},{1,3},{2,4},{3,5},{4,6},{5,7},{6,0},{7,1},{8,10},{9,11},{10,... | collective-permute-start | bytes 3145736 | tf_op jit(solution)/shard_map/ppermute | solution.py:42
  60.0 15.1 %collective-permute-start.14 = (bf16[256,1024]{1,0:T(8,128)(2,1)S(1)}, bf16[256,1024]{1,0:T(8,128)(2,1)S(1)}, u32[]{:S(2)}, u32[]{:S(2)}) collective-permute-start(bf16[256,1024]{1,0:T(8,128)(2,1)S(1)} %collective-permute-done.11.refs_0_), channel_id=1, source_target_pairs={{0,2},{1,3},{2,4},{3,5},{4,6},{5,7},{6,0},{7,1},{8,10},{9,11},{10,... | collective-permute-start | bytes 1572872 | tf_op jit(solution)/shard_map/ppermute | solution.py:42
  60.0 15.1 %collective-permute-start.16 = (bf16[256,1024]{1,0:T(8,128)(2,1)S(1)}, bf16[256,1024]{1,0:T(8,128)(2,1)S(1)}, u32[]{:S(2)}, u32[]{:S(2)}) collective-permute-start(bf16[256,1024]{1,0:T(8,128)(2,1)S(1)} %collective-permute-done.15.refs_2_), channel_id=1, source_target_pairs={{0,6},{1,7},{2,0},{3,1},{4,2},{5,3},{6,4},{7,5},{8,14},{9,15},{10,... | collective-permute-start | bytes 1572872 | tf_op jit(solution)/shard_map/ppermute | solution.py:42
  65.6 13.0 %collective-permute-start.13 = (bf16[256,1024]{1,0:T(8,128)(2,1)S(1)}, bf16[256,1024]{1,0:T(8,128)(2,1)S(1)}, u32[]{:S(2)}, u32[]{:S(2)}) collective-permute-start(bf16[256,1024]{1,0:T(8,128)(2,1)S(1)} %collective-permute-done.12.refs_1_), channel_id=1, source_target_pairs={{0,6},{1,7},{2,0},{3,1},{4,2},{5,3},{6,4},{7,5},{8,14},{9,15},{10,... | collective-permute-start | bytes 1572872 | tf_op jit(solution)/shard_map/ppermute | solution.py:42
  80.4 8.8 %collective-permute-start.19 = (bf16[512,1024]{1,0:T(8,128)(2,1)S(1)}, bf16[512,1024]{1,0:T(8,128)(2,1)S(1)}, u32[]{:S(2)}, u32[]{:S(2)}) collective-permute-start(bf16[512,1024]{1,0:T(8,128)(2,1)S(1)} %shard_map.65), channel_id=1, source_target_pairs={{0,32},{1,33},{2,34},{3,35},{4,36},{5,37},{6,38},{7,39},{8,40},{9,... | collective-permute-start | bytes 3145736 | tf_op jit(solution)/shard_map/ppermute | solution.py:42
